TPU v7x, 32 devices: a whole 2x2x4 slice. The times are simulated.
32 devices in a mesh: fsdp: 32 (over z, y, x, core).
Axes of the slice: x: 2, y: 2, z: 4, core: 2. Of those that a mesh axis runs over, the one named last changes fastest.
Arguments:
- latents: float32 [128, 256, 16], P('fsdp'), may hold values from -6 to 6
- noise: float32 [128, 256, 16], P('fsdp'), may hold values from -6 to 6
- timesteps: int32 [128], P('fsdp'), may hold values from 0 to 999
- labels: int32 [128], P('fsdp'), may hold values from 0 to 999
- qkv_weight: float32 [2, 768, 2304], P(None, 'fsdp'), may hold values from -0.21875 to 0.21875
- proj_weight: float32 [2, 768, 768], P(None, 'fsdp'), may hold values from -0.875 to 0.875
- up_weight: float32 [2, 768, 3072], P(None, 'fsdp'), may hold values from -0.21875 to 0.21875
- down_weight: float32 [2, 3072, 768], P(None, 'fsdp'), may hold values from -0.109375 to 0.109375
- mod_weight: float32 [768, 10752], P('fsdp'), may hold values from -0.21875 to 0.21875
- tables: float32 [2056, 768], P(None, 'fsdp'), may hold values from -4 to 4
- biases: float32 [25360], replicated, may hold values from -4 to 4
- qkv_first: float32 [2, 768, 2304], P(None, 'fsdp'), may hold values from -0.00030517578 to 0.00030517578
- proj_first: float32 [2, 768, 768], P(None, 'fsdp'), may hold values from -0.00030517578 to 0.00030517578
- up_first: float32 [2, 768, 3072], P(None, 'fsdp'), may hold values from -0.00030517578 to 0.00030517578
- down_first: float32 [2, 3072, 768], P(None, 'fsdp'), may hold values from -0.00030517578 to 0.00030517578
- mod_first: float32 [768, 10752], P('fsdp'), may hold values from -0.00030517578 to 0.00030517578
- tables_first: float32 [2056, 768], P(None, 'fsdp'), may hold values from -0.00030517578 to 0.00030517578
- biases_first: float32 [25360], replicated, may hold values from -0.00030517578 to 0.00030517578
- qkv_second: float32 [2, 768, 2304], P(None, 'fsdp'), may hold values from 3e-09 to 5e-08
- proj_second: float32 [2, 768, 768], P(None, 'fsdp'), may hold values from 3e-09 to 5e-08
- up_second: float32 [2, 768, 3072], P(None, 'fsdp'), may hold values from 3e-09 to 5e-08
- down_second: float32 [2, 3072, 768], P(None, 'fsdp'), may hold values from 3e-09 to 5e-08
- mod_second: float32 [768, 10752], P('fsdp'), may hold values from 3e-09 to 5e-08
- tables_second: float32 [2056, 768], P(None, 'fsdp'), may hold values from 3e-09 to 5e-08
- biases_second: float32 [25360], replicated, may hold values from 3e-09 to 5e-08
Outputs:
- loss_value: float32 [], replicated
- grad_norm: float32 [], replicated
- qkv_update: float32 [2, 768, 2304], P(None, 'fsdp')
- qkv_first_new: float32 [2, 768, 2304], P(None, 'fsdp')
- qkv_second_new: float32 [2, 768, 2304], P(None, 'fsdp')
- proj_update: float32 [2, 768, 768], P(None, 'fsdp')
- proj_first_new: float32 [2, 768, 768], P(None, 'fsdp')
- proj_second_new: float32 [2, 768, 768], P(None, 'fsdp')
- up_update: float32 [2, 768, 3072], P(None, 'fsdp')
- up_first_new: float32 [2, 768, 3072], P(None, 'fsdp')
- up_second_new: float32 [2, 768, 3072], P(None, 'fsdp')
- down_update: float32 [2, 3072, 768], P(None, 'fsdp')
- down_first_new: float32 [2, 3072, 768], P(None, 'fsdp')
- down_second_new: float32 [2, 3072, 768], P(None, 'fsdp')
- mod_update: float32 [768, 10752], P('fsdp')
- mod_first_new: float32 [768, 10752], P('fsdp')
- mod_second_new: float32 [768, 10752], P('fsdp')
- tables_update: float32 [2056, 768], P(None, 'fsdp')
- tables_first_new: float32 [2056, 768], P(None, 'fsdp')
- tables_second_new: float32 [2056, 768], P(None, 'fsdp')
- biases_update: float32 [25360], replicated
- biases_first_new: float32 [25360], replicated
- biases_second_new: float32 [25360], replicated
All inputs are finite; a program needn't handle non-finite values.
Results may differ from a plain program's by a relative error of at most 0.011.
Values may be sent and summed in bfloat16 or wider, within the bound.
No kernel may reach another device: no remote copies, remote signals or barrier semaphores. Data moves between devices by JAX's collectives and lax.ppermute only.
A program may use at most 384 MiB of HBM per device.

v0:
```python
import math

import jax
import jax.numpy as jnp
from jax import lax
from jax.sharding import PartitionSpec as P

D = 768
HEADS = 12
HD = 64
FF = 3072
FREQ = 256
CLASSES = 1000
DIFF_STEPS = 1000
LAYERS = 2
MICRO = 2
TOK = 256
PD = 16
MODW = 10752


norm_eps = 1e-06
clip_limit = 2.5
learn_rate = 0.01
beta_first = 0.9
beta_second = 0.95
adam_eps = 1e-08
weight_decay = 0.01
first_fix = 1.0 - 0.9**10
second_fix = 1.0 - 0.95**10


def modulate(residual, shift_term, scale_term):
    centred = residual - jnp.mean(residual, axis=-1, keepdims=True)
    spread = jnp.mean(centred * centred, axis=-1, keepdims=True)
    normed = centred * lax.rsqrt(spread + norm_eps)
    return normed * (1.0 + scale_term[:, None, :]) + shift_term[:, None, :]


def gelu_tanh(values):
    return jax.nn.gelu(values, approximate=True)


def product(left_side, right_side):
    return jnp.dot(left_side, right_side, preferred_element_type=jnp.float32)


def left_product(left_side, right_side):
    return lax.dot_general(
        left_side, right_side, (((0,), (0,)), ((), ())), preferred_element_type=jnp.float32
    )


def right_product(left_side, right_side):
    return lax.dot_general(
        left_side, right_side, (((1,), (1,)), ((), ())), preferred_element_type=jnp.float32
    )


def time_features(steps_in):
    half_count = FREQ // 2
    frequencies = jnp.exp(
        -math.log(10000.0) * jnp.arange(half_count, dtype=jnp.float32) / half_count
    )
    angles = steps_in.astype(jnp.float32)[:, None] * frequencies[None, :]
    return jnp.concatenate([jnp.cos(angles), jnp.sin(angles)], axis=1)


def noise_share(steps_in):
    beta_values = jnp.linspace(0.0001, 0.02, DIFF_STEPS, dtype=jnp.float32)
    log_keep = jnp.cumsum(jnp.log(1.0 - beta_values))
    return jnp.exp(jnp.take(log_keep, steps_in))


def bias_parts(biases):
    per_layer = 10 * D + FF
    layer_parts = []
    for layer_index in range(LAYERS):
        anchor = layer_index * per_layer
        layer_parts.append(
            (
                biases[anchor : anchor + D],
                biases[anchor + D : anchor + 2 * D],
                biases[anchor + 2 * D : anchor + 3 * D],
                biases[anchor + 3 * D : anchor + 3 * D + FF],
                biases[anchor + 3 * D + FF : anchor + 4 * D + FF],
                biases[anchor + 4 * D + FF : anchor + per_layer],
            )
        )
    anchor = LAYERS * per_layer
    global_parts = (
        biases[anchor : anchor + 2 * D],
        biases[anchor + 2 * D : anchor + 3 * D],
        biases[anchor + 3 * D : anchor + 4 * D],
        biases[anchor + 4 * D : anchor + 5 * D],
        biases[anchor + 5 * D : anchor + 5 * D + PD],
    )
    return (layer_parts, global_parts)


def split_heads(packed_low, sample_count):
    queries = packed_low[:, :D].reshape(sample_count, TOK, HEADS, HD)
    keys_all = packed_low[:, D : 2 * D].reshape(sample_count, TOK, HEADS, HD)
    values_all = packed_low[:, 2 * D :].reshape(sample_count, TOK, HEADS, HD)
    return (queries, keys_all, values_all)


def attention_forward(packed_low, sample_count):
    queries, keys_all, values_all = split_heads(packed_low, sample_count)
    scores = jnp.einsum(
        "bqhd,bkhd->bhqk", queries, keys_all, preferred_element_type=jnp.float32
    ) * HD ** (-0.5)
    row_max = jnp.max(scores, axis=-1, keepdims=True)
    log_total = row_max + jnp.log(jnp.sum(jnp.exp(scores - row_max), axis=-1, keepdims=True))
    soft_low = jnp.exp(scores - log_total).astype(jnp.bfloat16)
    mixed = jnp.einsum("bhqk,bkhd->bqhd", soft_low, values_all, preferred_element_type=jnp.float32)
    return (mixed.reshape(sample_count * TOK, D), log_total)


def attention_backward(packed_low, log_total, grad_mixed_low, sample_count):
    queries, keys_all, values_all = split_heads(packed_low, sample_count)
    scores = jnp.einsum(
        "bqhd,bkhd->bhqk", queries, keys_all, preferred_element_type=jnp.float32
    ) * HD ** (-0.5)
    soft_weights = jnp.exp(scores - log_total)
    soft_low = soft_weights.astype(jnp.bfloat16)
    grad_mix = grad_mixed_low.reshape(sample_count, TOK, HEADS, HD)
    grad_values = jnp.einsum(
        "bhqk,bqhd->bkhd", soft_low, grad_mix, preferred_element_type=jnp.float32
    )
    grad_soft = jnp.einsum(
        "bqhd,bkhd->bhqk", grad_mix, values_all, preferred_element_type=jnp.float32
    )
    grad_scores = soft_weights * (
        grad_soft - jnp.sum(soft_weights * grad_soft, axis=-1, keepdims=True)
    )
    score_low = grad_scores.astype(jnp.bfloat16)
    grad_queries = jnp.einsum(
        "bhqk,bkhd->bqhd", score_low, keys_all, preferred_element_type=jnp.float32
    ) * HD ** (-0.5)
    grad_keys = jnp.einsum(
        "bhqk,bqhd->bkhd", score_low, queries, preferred_element_type=jnp.float32
    ) * HD ** (-0.5)
    row_count = sample_count * TOK
    return jnp.concatenate(
        [
            grad_queries.reshape(row_count, D),
            grad_keys.reshape(row_count, D),
            grad_values.reshape(row_count, D),
        ],
        axis=1,
    )


def adam_step(weight_now, grad_now, first_old, second_old, factor):
    clipped = grad_now * factor
    first_new = beta_first * first_old + (1.0 - beta_first) * clipped
    second_new = beta_second * second_old + (1.0 - beta_second) * clipped * clipped
    step_size = -learn_rate * (
        first_new / first_fix / (jnp.sqrt(second_new / second_fix) + adam_eps)
        + weight_decay * weight_now
    )
    return (step_size, first_new, second_new)


def body(
    latents,
    noise,
    timesteps,
    labels,
    qkv_weight,
    proj_weight,
    up_weight,
    down_weight,
    mod_weight,
    tables,
    biases,
    qkv_first,
    proj_first,
    up_first,
    down_first,
    mod_first,
    tables_first,
    biases_first,
    qkv_second,
    proj_second,
    up_second,
    down_second,
    mod_second,
    tables_second,
    biases_second,
):
    local_count = latents.shape[0]
    per_batch = local_count // MICRO
    row_count = per_batch * TOK
    total_count = local_count * lax.axis_size("fsdp") * TOK * PD
    qkv_low = qkv_weight.astype(jnp.bfloat16)
    proj_low = proj_weight.astype(jnp.bfloat16)
    up_low = up_weight.astype(jnp.bfloat16)
    down_low = down_weight.astype(jnp.bfloat16)
    mod_low = mod_weight.astype(jnp.bfloat16)
    tables_low = tables.astype(jnp.bfloat16)
    layer_parts, global_parts = bias_parts(biases)
    final_bias, patch_bias, first_bias, second_bias, head_bias = global_parts
    mod_bias = jnp.concatenate([part_item[5] for part_item in layer_parts] + [final_bias])
    zeros_f32 = jnp.float32
    grad_qkv = [jnp.zeros((D, 3 * D), zeros_f32) for layer_index in range(LAYERS)]
    grad_proj = [jnp.zeros((D, D), zeros_f32) for layer_index in range(LAYERS)]
    grad_up = [jnp.zeros((D, FF), zeros_f32) for layer_index in range(LAYERS)]
    grad_down = [jnp.zeros((FF, D), zeros_f32) for layer_index in range(LAYERS)]
    grad_query_bias = [jnp.zeros((D,), zeros_f32) for layer_index in range(LAYERS)]
    grad_value_bias = [jnp.zeros((D,), zeros_f32) for layer_index in range(LAYERS)]
    grad_proj_bias = [jnp.zeros((D,), zeros_f32) for layer_index in range(LAYERS)]
    grad_up_bias = [jnp.zeros((FF,), zeros_f32) for layer_index in range(LAYERS)]
    grad_down_bias = [jnp.zeros((D,), zeros_f32) for layer_index in range(LAYERS)]
    grad_mod = jnp.zeros((D, MODW), zeros_f32)
    grad_mod_bias = jnp.zeros((MODW,), zeros_f32)
    grad_patch = jnp.zeros((PD, D), zeros_f32)
    grad_first = jnp.zeros((FREQ, D), zeros_f32)
    grad_second = jnp.zeros((D, D), zeros_f32)
    grad_class = jnp.zeros((CLASSES, D), zeros_f32)
    grad_head = jnp.zeros((PD, D), zeros_f32)
    grad_patch_bias = jnp.zeros((D,), zeros_f32)
    grad_first_bias = jnp.zeros((D,), zeros_f32)
    grad_second_bias = jnp.zeros((D,), zeros_f32)
    grad_head_bias = jnp.zeros((PD,), zeros_f32)
    loss_local = jnp.zeros((), zeros_f32)
    for batch_index in range(MICRO):
        first_sample = batch_index * per_batch
        batch_latents = latents[first_sample : first_sample + per_batch]
        batch_noise = noise[first_sample : first_sample + per_batch]
        batch_steps = timesteps[first_sample : first_sample + per_batch]
        batch_labels = labels[first_sample : first_sample + per_batch]
        tables_full, mod_full = (
            lax.all_gather(tables_low, "fsdp", axis=1, tiled=True),
            lax.all_gather(mod_low, "fsdp", axis=0, tiled=True),
        )
        patch_rows = tables_full[:PD]
        first_rows = tables_full[PD : PD + FREQ]
        second_rows = tables_full[PD + FREQ : PD + FREQ + D]
        class_rows = tables_full[PD + FREQ + D : PD + FREQ + D + CLASSES]
        head_rows = tables_full[PD + FREQ + D + CLASSES :]
        keep_share = noise_share(batch_steps)
        noised = (
            jnp.sqrt(keep_share)[:, None, None] * batch_latents
            + jnp.sqrt(1.0 - keep_share)[:, None, None] * batch_noise
        )
        noised_low = noised.reshape(row_count, PD).astype(jnp.bfloat16)
        residual = (product(noised_low, patch_rows) + patch_bias).reshape(per_batch, TOK, D)
        features_low = time_features(batch_steps).astype(jnp.bfloat16)
        first_pre = product(features_low, first_rows) + first_bias
        first_low = jax.nn.silu(first_pre).astype(jnp.bfloat16)
        time_embed = product(first_low, second_rows) + second_bias
        condition = time_embed + jnp.take(class_rows, batch_labels, axis=0).astype(jnp.float32)
        cond_low = jax.nn.silu(condition).astype(jnp.bfloat16)
        modulations = product(cond_low, mod_full) + mod_bias
        stored = []
        for layer_index in range(LAYERS):
            qkv_full, proj_full, up_full, down_full = (
                lax.all_gather(qkv_low[layer_index], "fsdp", axis=0, tiled=True),
                lax.all_gather(proj_low[layer_index], "fsdp", axis=0, tiled=True),
                lax.all_gather(up_low[layer_index], "fsdp", axis=0, tiled=True),
                lax.all_gather(down_low[layer_index], "fsdp", axis=0, tiled=True),
            )
            query_bias, value_bias, proj_bias, up_bias, down_bias, unused = layer_parts[layer_index]
            segment = modulations[:, layer_index * 6 * D : (layer_index + 1) * 6 * D]
            mod_terms = [
                segment[:, part_index * D : (part_index + 1) * D] for part_index in range(6)
            ]
            shift_attn, scale_attn, gate_attn, shift_mlp, scale_mlp, gate_mlp = mod_terms
            residual_in = residual
            hidden_low = (
                modulate(residual_in, shift_attn, scale_attn)
                .reshape(row_count, D)
                .astype(jnp.bfloat16)
            )
            packed_bias = jnp.concatenate([query_bias, jnp.zeros((D,), jnp.float32), value_bias])
            packed_low = (product(hidden_low, qkv_full) + packed_bias).astype(jnp.bfloat16)
            mixed, log_total = attention_forward(packed_low, per_batch)
            mixed_low = mixed.astype(jnp.bfloat16)
            attn_out = (product(mixed_low, proj_full) + proj_bias).reshape(per_batch, TOK, D)
            residual_mid = residual_in + gate_attn[:, None, :] * attn_out
            hidden_two_low = (
                modulate(residual_mid, shift_mlp, scale_mlp)
                .reshape(row_count, D)
                .astype(jnp.bfloat16)
            )
            pre_act = product(hidden_two_low, up_full) + up_bias
            act_low = gelu_tanh(pre_act).astype(jnp.bfloat16)
            mlp_out = (product(act_low, down_full) + down_bias).reshape(per_batch, TOK, D)
            residual = residual_mid + gate_mlp[:, None, :] * mlp_out
            stored.append(
                (
                    residual_in,
                    hidden_low,
                    packed_low,
                    log_total,
                    mixed_low,
                    attn_out,
                    residual_mid,
                    hidden_two_low,
                    pre_act,
                    act_low,
                    mlp_out,
                )
            )
        final_mods = modulations[:, LAYERS * 6 * D :]
        final_hidden = modulate(residual, final_mods[:, :D], final_mods[:, D:])
        final_low = final_hidden.reshape(row_count, D).astype(jnp.bfloat16)
        predicted = right_product(final_low, head_rows) + head_bias
        errors = predicted - batch_noise.reshape(row_count, PD)
        loss_local = loss_local + jnp.sum(errors * errors) / total_count
        tables_full, mod_full = (
            lax.all_gather(tables_low, "fsdp", axis=1, tiled=True),
            lax.all_gather(mod_low, "fsdp", axis=0, tiled=True),
        )
        second_rows = tables_full[PD + FREQ : PD + FREQ + D]
        head_rows = tables_full[PD + FREQ + D + CLASSES :]
        grad_pred_low = (2.0 * errors / total_count).astype(jnp.bfloat16)
        grad_head_bias = grad_head_bias + jnp.sum(grad_pred_low.astype(jnp.float32), axis=0)
        grad_head = grad_head + left_product(grad_pred_low, final_low)
        grad_final = product(grad_pred_low, head_rows).reshape(per_batch, TOK, D)
        unused, final_pull = jax.vjp(modulate, residual, final_mods[:, :D], final_mods[:, D:])
        grad_residual, grad_shift_final, grad_scale_final = final_pull(grad_final)
        mod_grads = [None] * LAYERS
        for layer_index in reversed(range(LAYERS)):
            qkv_full, proj_full, up_full, down_full = (
                lax.all_gather(qkv_low[layer_index], "fsdp", axis=0, tiled=True),
                lax.all_gather(proj_low[layer_index], "fsdp", axis=0, tiled=True),
                lax.all_gather(up_low[layer_index], "fsdp", axis=0, tiled=True),
                lax.all_gather(down_low[layer_index], "fsdp", axis=0, tiled=True),
            )
            (
                residual_in,
                hidden_low,
                packed_low,
                log_total,
                mixed_low,
                attn_out,
                residual_mid,
                hidden_two_low,
                pre_act,
                act_low,
                mlp_out,
            ) = stored[layer_index]
            segment = modulations[:, layer_index * 6 * D : (layer_index + 1) * 6 * D]
            mod_terms = [
                segment[:, part_index * D : (part_index + 1) * D] for part_index in range(6)
            ]
            shift_attn, scale_attn, gate_attn, shift_mlp, scale_mlp, gate_mlp = mod_terms
            grad_gate_mlp = jnp.sum(grad_residual * mlp_out, axis=1)
            grad_mlp_low = (
                (grad_residual * gate_mlp[:, None, :]).reshape(row_count, D).astype(jnp.bfloat16)
            )
            grad_down_bias[layer_index] = grad_down_bias[layer_index] + jnp.sum(
                grad_mlp_low.astype(jnp.float32), axis=0
            )
            grad_down[layer_index] = grad_down[layer_index] + left_product(act_low, grad_mlp_low)
            grad_act = right_product(grad_mlp_low, down_full)
            unused, gelu_pull = jax.vjp(gelu_tanh, pre_act)
            grad_pre_low = gelu_pull(grad_act)[0].astype(jnp.bfloat16)
            grad_up_bias[layer_index] = grad_up_bias[layer_index] + jnp.sum(
                grad_pre_low.astype(jnp.float32), axis=0
            )
            grad_up[layer_index] = grad_up[layer_index] + left_product(hidden_two_low, grad_pre_low)
            grad_hidden_two = right_product(grad_pre_low, up_full).reshape(per_batch, TOK, D)
            unused, mlp_pull = jax.vjp(modulate, residual_mid, shift_mlp, scale_mlp)
            part_residual, grad_shift_mlp, grad_scale_mlp = mlp_pull(grad_hidden_two)
            grad_residual = grad_residual + part_residual
            grad_gate_attn = jnp.sum(grad_residual * attn_out, axis=1)
            grad_attn_low = (
                (grad_residual * gate_attn[:, None, :]).reshape(row_count, D).astype(jnp.bfloat16)
            )
            grad_proj_bias[layer_index] = grad_proj_bias[layer_index] + jnp.sum(
                grad_attn_low.astype(jnp.float32), axis=0
            )
            grad_proj[layer_index] = grad_proj[layer_index] + left_product(mixed_low, grad_attn_low)
            grad_mixed_low = right_product(grad_attn_low, proj_full).astype(jnp.bfloat16)
            grad_packed_low = attention_backward(
                packed_low, log_total, grad_mixed_low, per_batch
            ).astype(jnp.bfloat16)
            grad_packed = grad_packed_low.astype(jnp.float32)
            grad_query_bias[layer_index] = grad_query_bias[layer_index] + jnp.sum(
                grad_packed[:, :D], axis=0
            )
            grad_value_bias[layer_index] = grad_value_bias[layer_index] + jnp.sum(
                grad_packed[:, 2 * D :], axis=0
            )
            grad_qkv[layer_index] = grad_qkv[layer_index] + left_product(
                hidden_low, grad_packed_low
            )
            grad_hidden = right_product(grad_packed_low, qkv_full).reshape(per_batch, TOK, D)
            unused, attn_pull = jax.vjp(modulate, residual_in, shift_attn, scale_attn)
            part_residual, grad_shift_attn, grad_scale_attn = attn_pull(grad_hidden)
            grad_residual = grad_residual + part_residual
            mod_grads[layer_index] = jnp.concatenate(
                [
                    grad_shift_attn,
                    grad_scale_attn,
                    grad_gate_attn,
                    grad_shift_mlp,
                    grad_scale_mlp,
                    grad_gate_mlp,
                ],
                axis=1,
            )
        grad_zero_low = grad_residual.reshape(row_count, D).astype(jnp.bfloat16)
        grad_patch_bias = grad_patch_bias + jnp.sum(grad_zero_low.astype(jnp.float32), axis=0)
        grad_patch = grad_patch + left_product(noised_low, grad_zero_low)
        grad_mods_low = jnp.concatenate(
            mod_grads + [grad_shift_final, grad_scale_final], axis=1
        ).astype(jnp.bfloat16)
        grad_mod_bias = grad_mod_bias + jnp.sum(grad_mods_low.astype(jnp.float32), axis=0)
        grad_mod = grad_mod + left_product(cond_low, grad_mods_low)
        grad_cond_act = right_product(grad_mods_low, mod_full)
        unused, silu_pull = jax.vjp(jax.nn.silu, condition)
        grad_condition = silu_pull(grad_cond_act)[0]
        grad_class = grad_class.at[batch_labels].add(grad_condition)
        grad_time_low = grad_condition.astype(jnp.bfloat16)
        grad_second_bias = grad_second_bias + jnp.sum(grad_time_low.astype(jnp.float32), axis=0)
        grad_second = grad_second + left_product(first_low, grad_time_low)
        grad_first_act = right_product(grad_time_low, second_rows)
        unused, first_pull = jax.vjp(jax.nn.silu, first_pre)
        grad_first_low = first_pull(grad_first_act)[0].astype(jnp.bfloat16)
        grad_first_bias = grad_first_bias + jnp.sum(grad_first_low.astype(jnp.float32), axis=0)
        grad_first = grad_first + left_product(features_low, grad_first_low)
    grad_tables = jnp.concatenate(
        [grad_patch, grad_first, grad_second, grad_class, grad_head], axis=0
    )
    shard_qkv, shard_proj, shard_up, shard_down, shard_mod, shard_tables = (
        lax.psum_scatter(jnp.stack(grad_qkv), "fsdp", scatter_dimension=1, tiled=True),
        lax.psum_scatter(jnp.stack(grad_proj), "fsdp", scatter_dimension=1, tiled=True),
        lax.psum_scatter(jnp.stack(grad_up), "fsdp", scatter_dimension=1, tiled=True),
        lax.psum_scatter(jnp.stack(grad_down), "fsdp", scatter_dimension=1, tiled=True),
        lax.psum_scatter(grad_mod, "fsdp", scatter_dimension=0, tiled=True),
        lax.psum_scatter(grad_tables, "fsdp", scatter_dimension=1, tiled=True),
    )
    pieces = []
    for layer_index in range(LAYERS):
        pieces += [
            grad_query_bias[layer_index],
            grad_value_bias[layer_index],
            grad_proj_bias[layer_index],
            grad_up_bias[layer_index],
            grad_down_bias[layer_index],
            grad_mod_bias[layer_index * 6 * D : (layer_index + 1) * 6 * D],
        ]
    pieces += [
        grad_mod_bias[LAYERS * 6 * D :],
        grad_patch_bias,
        grad_first_bias,
        grad_second_bias,
        grad_head_bias,
    ]
    bias_local = jnp.concatenate(pieces)
    shard_squares = (
        jnp.sum(shard_qkv * shard_qkv)
        + jnp.sum(shard_proj * shard_proj)
        + jnp.sum(shard_up * shard_up)
        + jnp.sum(shard_down * shard_down)
        + jnp.sum(shard_mod * shard_mod)
        + jnp.sum(shard_tables * shard_tables)
    )
    bias_grad, square_total, loss_value = lax.psum((bias_local, shard_squares, loss_local), "fsdp")
    grad_norm = jnp.sqrt(square_total + jnp.sum(bias_grad * bias_grad))
    factor = jnp.minimum(1.0, clip_limit / (grad_norm + 1e-06))
    qkv_update, qkv_first_new, qkv_second_new = adam_step(
        qkv_weight, shard_qkv, qkv_first, qkv_second, factor
    )
    proj_update, proj_first_new, proj_second_new = adam_step(
        proj_weight, shard_proj, proj_first, proj_second, factor
    )
    up_update, up_first_new, up_second_new = adam_step(
        up_weight, shard_up, up_first, up_second, factor
    )
    down_update, down_first_new, down_second_new = adam_step(
        down_weight, shard_down, down_first, down_second, factor
    )
    mod_update, mod_first_new, mod_second_new = adam_step(
        mod_weight, shard_mod, mod_first, mod_second, factor
    )
    tables_update, tables_first_new, tables_second_new = adam_step(
        tables, shard_tables, tables_first, tables_second, factor
    )
    biases_update, biases_first_new, biases_second_new = adam_step(
        biases, bias_grad, biases_first, biases_second, factor
    )
    return (
        loss_value,
        grad_norm,
        qkv_update,
        qkv_first_new,
        qkv_second_new,
        proj_update,
        proj_first_new,
        proj_second_new,
        up_update,
        up_first_new,
        up_second_new,
        down_update,
        down_first_new,
        down_second_new,
        mod_update,
        mod_first_new,
        mod_second_new,
        tables_update,
        tables_first_new,
        tables_second_new,
        biases_update,
        biases_first_new,
        biases_second_new,
    )


def solution(mesh):
    in_specs = (
        P("fsdp", None, None),
        P("fsdp", None, None),
        P("fsdp"),
        P("fsdp"),
        P(None, "fsdp", None),
        P(None, "fsdp", None),
        P(None, "fsdp", None),
        P(None, "fsdp", None),
        P("fsdp", None),
        P(None, "fsdp"),
        P(),
        P(None, "fsdp", None),
        P(None, "fsdp", None),
        P(None, "fsdp", None),
        P(None, "fsdp", None),
        P("fsdp", None),
        P(None, "fsdp"),
        P(),
        P(None, "fsdp", None),
        P(None, "fsdp", None),
        P(None, "fsdp", None),
        P(None, "fsdp", None),
        P("fsdp", None),
        P(None, "fsdp"),
        P(),
    )
    out_specs = (
        P(),
        P(),
        P(None, "fsdp", None),
        P(None, "fsdp", None),
        P(None, "fsdp", None),
        P(None, "fsdp", None),
        P(None, "fsdp", None),
        P(None, "fsdp", None),
        P(None, "fsdp", None),
        P(None, "fsdp", None),
        P(None, "fsdp", None),
        P(None, "fsdp", None),
        P(None, "fsdp", None),
        P(None, "fsdp", None),
        P("fsdp", None),
        P("fsdp", None),
        P("fsdp", None),
        P(None, "fsdp"),
        P(None, "fsdp"),
        P(None, "fsdp"),
        P(),
        P(),
        P(),
    )
    return jax.shard_map(body, mesh=mesh, in_specs=in_specs, out_specs=out_specs, check_vma=False)
```

profile of v0, /device:TPU:0, one launch (start us, length us, event | category | flops | bytes accessed | tf_op | source)
XLA Modules:
  0.0 2302.3 jit_solution(14887553259606947400)
XLA Ops:
  21.7 52.2 %all-gather.19.cloned.1.call-done = bf16[2056,768]{0,1:T(8,128)(2,1)} async-done(((bf16[2056,24]{0,1:T(8,128)(2,1)}), bf16[2056,768]{0,1:T(8,128)(2,1)}) %all-gather.19.cloned.1.call-update) | async-done | bytes 3158032 | tf_op jit(solution)/shard_map/all_gather | solution.py:235
  97.4 92.0 %all-gather.21.cloned.1.call-done = bf16[768,10752]{1,0:T(8,128)(2,1)} async-done(((bf16[24,10752]{1,0:T(8,128)(2,1)}), bf16[768,10752]{1,0:T(8,128)(2,1)}) %all-gather.21.cloned.1.call-update) | async-done | bytes 16515088 | tf_op jit(solution)/shard_map/all_gather | solution.py:236
  197.9 53.3 %all-gather.23.cloned.1.call-done = bf16[1,768,2304]{2,1,0:T(8,128)(2,1)} async-done(((bf16[1,24,2304]{2,1,0:T(8,128)(2,1)}), bf16[1,768,2304]{2,1,0:T(8,128)(2,1)}) %all-gather.23.cloned.1.call-update) | async-done | bytes 3538960 | tf_op jit(solution)/shard_map/all_gather | solution.py:260
  276.8 30.5 %all-gather.25.cloned.1.call-done = bf16[1,768,768]{2,1,0:T(8,128)(2,1)} async-done(((bf16[1,24,768]{2,1,0:T(8,128)(2,1)}), bf16[1,768,768]{2,1,0:T(8,128)(2,1)}) %all-gather.25.cloned.1.call-update) | async-done | bytes 1179664 | tf_op jit(solution)/shard_map/all_gather | solution.py:261
  312.2 60.9 %all-gather.27.cloned.1.call-done = bf16[1,768,3072]{2,1,0:T(8,128)(2,1)} async-done(((bf16[1,24,3072]{2,1,0:T(8,128)(2,1)}), bf16[1,768,3072]{2,1,0:T(8,128)(2,1)}) %all-gather.27.cloned.1.call-update) | async-done | bytes 4718608 | tf_op jit(solution)/shard_map/all_gather | solution.py:262
  380.1 58.3 %all-gather.29.cloned.1.call-done = bf16[1,3072,768]{2,1,0:T(8,128)(2,1)} async-done(((bf16[1,96,768]{2,1,0:T(8,128)(2,1)}), bf16[1,3072,768]{2,1,0:T(8,128)(2,1)}) %all-gather.29.cloned.1.call-update) | async-done | bytes 4718608 | tf_op jit(solution)/shard_map/all_gather | solution.py:263
  449.2 50.9 %all-gather.31.cloned.1.call-done = bf16[1,768,2304]{2,1,0:T(8,128)(2,1)} async-done(((bf16[1,24,2304]{2,1,0:T(8,128)(2,1)}), bf16[1,768,2304]{2,1,0:T(8,128)(2,1)}) %all-gather.31.cloned.1.call-update) | async-done | bytes 3538960 | tf_op jit(solution)/shard_map/all_gather | solution.py:260
  526.1 30.2 %all-gather.33.cloned.1.call-done = bf16[1,768,768]{2,1,0:T(8,128)(2,1)} async-done(((bf16[1,24,768]{2,1,0:T(8,128)(2,1)}), bf16[1,768,768]{2,1,0:T(8,128)(2,1)}) %all-gather.33.cloned.1.call-update) | async-done | bytes 1179664 | tf_op jit(solution)/shard_map/all_gather | solution.py:261
  561.2 61.2 %all-gather.35.cloned.1.call-done = bf16[1,768,3072]{2,1,0:T(8,128)(2,1)} async-done(((bf16[1,24,3072]{2,1,0:T(8,128)(2,1)}), bf16[1,768,3072]{2,1,0:T(8,128)(2,1)}) %all-gather.35.cloned.1.call-update) | async-done | bytes 4718608 | tf_op jit(solution)/shard_map/all_gather | solution.py:262
  629.2 58.4 %all-gather.37.cloned.1.call-done = bf16[1,3072,768]{2,1,0:T(8,128)(2,1)} async-done(((bf16[1,96,768]{2,1,0:T(8,128)(2,1)}), bf16[1,3072,768]{2,1,0:T(8,128)(2,1)}) %all-gather.37.cloned.1.call-update) | async-done | bytes 4718608 | tf_op jit(solution)/shard_map/all_gather | solution.py:263
  712.5 10.2 convert_reduce_fusion
  1032.7 10.2 convert_reduce_fusion.18
  1079.6 11.2 pad_maximum_fusion.2
  1114.5 10.4 fusion.323
  1125.0 10.5 fusion.324
  1150.8 11.2 pad_maximum_fusion.1
  1162.8 13.9 fusion.322
  1176.7 25.6 %convolution_add_fusion = f32[768,10752]{1,0:T(8,128)} fusion(f32[768,10752]{1,0:T(8,128)} %fusion.322, bf16[2,10752]{1,0:T(2,128)(2,1)S(1)} %copy-done.176, f32[2,768]{1,0:T(2,128)S(1)} %copy-done.214), kind=kOutput, calls=%fused_computation.6 | convolution fusion | flops 41295360 | bytes 66109440 | tf_op jit(solution)/shard_map/dot_general | solution.py:49
  1215.0 109.1 %reduce-scatter.9.cloned.1.call-done = f32[2,24,768]{2,1,0:T(8,128)} async-done(((f32[2,768,768]{2,1,0:T(8,128)}), f32[2,24,768]{2,1,0:T(8,128)}) %reduce-scatter.9.cloned.1.call-update) | async-done | bytes 147472 | tf_op jit(solution)/shard_map/reduce_scatter | solution.py:432
  1325.7 166.4 %reduce-scatter.7.cloned.1.call-done = f32[2,24,2304]{2,1,0:T(8,128)} async-done(((f32[2,768,2304]{2,1,0:T(8,128)}), f32[2,24,2304]{2,1,0:T(8,128)}) %reduce-scatter.7.cloned.1.call-update) | async-done | bytes 442384 | tf_op jit(solution)/shard_map/reduce_scatter | solution.py:431
  1495.1 207.4 %reduce-scatter.11.cloned.1.call-done = f32[2,24,3072]{2,1,0:T(8,128)} async-done(((f32[2,768,3072]{2,1,0:T(8,128)}), f32[2,24,3072]{2,1,0:T(8,128)}) %reduce-scatter.11.cloned.1.call-update) | async-done | bytes 589840 | tf_op jit(solution)/shard_map/reduce_scatter | solution.py:433
  1705.0 208.0 %reduce-scatter.13.cloned.1.call-done = f32[2,96,768]{2,1,0:T(8,128)} async-done(((f32[2,3072,768]{2,1,0:T(8,128)}), f32[2,96,768]{2,1,0:T(8,128)}) %reduce-scatter.13.cloned.1.call-update) | async-done | bytes 589840 | tf_op jit(solution)/shard_map/reduce_scatter | solution.py:434
  1915.5 321.6 %reduce-scatter.15.cloned.1.call-done = f32[24,10752]{1,0:T(8,128)} async-done(((f32[768,10752]{1,0:T(8,128)}), f32[24,10752]{1,0:T(8,128)}) %reduce-scatter.15.cloned.1.call-update) | async-done | bytes 1032208 | tf_op jit(solution)/shard_map/reduce_scatter | solution.py:435
  2240.9 39.8 %all-reduce.2 = (f32[]{:T(128)}, f32[]{:T(128)}) all-reduce(f32[]{:T(128)S(6)} %add.1202, f32[]{:T(128)S(6)} %add.1252), channel_id=1, replica_groups=mesh['fsdp'=32] {'fsdp'}, use_global_device_ids=true, to_apply=%region_32.36 | all-reduce | flops 2 | bytes 16 | tf_op jit(solution)/shard_map/psum | solution.py:464
  (1100 shorter events, 572.3 us)
Async XLA Ops:
  7.2 66.7 %all-gather.19.cloned.1.call-start = ((), (), s32[]{:S(2)}) async-start(), calls=%async_computation.5 | async-start | bytes 3446784 | tf_op jit(solution)/shard_map/all_gather | solution.py:235
  9.0 180.4 %all-gather.21.cloned.1.call-start = ((), (), s32[]{:S(2)}) async-start(), calls=%async_computation.6 | async-start | bytes 17031168 | tf_op jit(solution)/shard_map/all_gather | solution.py:236
  11.2 240.0 %all-gather.23.cloned.1.call-start = ((), (), s32[]{:S(2)}) async-start(), calls=%async_computation.12 | async-start | bytes 3649536 | tf_op jit(solution)/shard_map/all_gather | solution.py:260
  12.0 295.2 %all-gather.25.cloned.1.call-start = ((), (), s32[]{:S(2)}) async-start(), calls=%async_computation.13 | async-start | bytes 1216512 | tf_op jit(solution)/shard_map/all_gather | solution.py:261
  12.8 360.3 %all-gather.27.cloned.1.call-start = ((), (), s32[]{:S(2)}) async-start(), calls=%async_computation.14 | async-start | bytes 4866048 | tf_op jit(solution)/shard_map/all_gather | solution.py:262
  13.6 424.7 %all-gather.29.cloned.1.call-start = ((), (), s32[]{:S(2)}) async-start(), calls=%async_computation.15 | async-start | bytes 4866048 | tf_op jit(solution)/shard_map/all_gather | solution.py:263
  14.5 485.6 %all-gather.31.cloned.1.call-start = ((), (), s32[]{:S(2)}) async-start(), calls=%async_computation.16 | async-start | bytes 3649536 | tf_op jit(solution)/shard_map/all_gather | solution.py:260
  15.2 541.1 %all-gather.33.cloned.1.call-start = ((), (), s32[]{:S(2)}) async-start(), calls=%async_computation.17 | async-start | bytes 1216512 | tf_op jit(solution)/shard_map/all_gather | solution.py:261
  16.0 606.3 %all-gather.35.cloned.1.call-start = ((), (), s32[]{:S(2)}) async-start(), calls=%async_computation.18 | async-start | bytes 4866048 | tf_op jit(solution)/shard_map/all_gather | solution.py:262
  16.7 670.9 %all-gather.37.cloned.1.call-start = ((), (), s32[]{:S(2)}) async-start(), calls=%async_computation.19 | async-start | bytes 4866048 | tf_op jit(solution)/shard_map/all_gather | solution.py:263
  17.3 1193.6 %all-reduce.6.cloned.1.call-start = ((), (), s32[]{:S(2)}) async-start(), calls=%async_computation.20 | async-start | bytes 12836864
  81.3 731.3 %copy-start.210 = (f32[512]{0:T(512)}, f32[512]{0:T(512)S(1)}, u32[]{:S(2)}) copy-start(f32[512]{0:T(512)S(1)} %broadcast_multiply_fusion.9) | copy-start | bytes 6148
  197.4 528.8 %copy-start.187 = (f32[2,768]{1,0:T(2,128)}, f32[2,768]{1,0:T(2,128)S(1)}, u32[]{:S(2)}) copy-start(f32[2,768]{1,0:T(2,128)S(1)} %get-tuple-element.274) | copy-start | bytes 18436
  197.4 529.4 %copy-start.200 = (f32[2,768]{1,0:T(2,128)}, f32[2,768]{1,0:T(2,128)S(1)}, u32[]{:S(2)}) copy-start(f32[2,768]{1,0:T(2,128)S(1)} %get-tuple-element.278) | copy-start | bytes 18436
  197.4 557.0 %copy-start.183 = (f32[2,768]{1,0:T(2,128)}, f32[2,768]{1,0:T(2,128)S(1)}, u32[]{:S(2)}) copy-start(f32[2,768]{1,0:T(2,128)S(1)} %get-tuple-element.277) | copy-start | bytes 18436
  197.5 557.7 %copy-start.202 = (f32[2,768]{1,0:T(2,128)}, f32[2,768]{1,0:T(2,128)S(1)}, u32[]{:S(2)}) copy-start(f32[2,768]{1,0:T(2,128)S(1)} %get-tuple-element.281) | copy-start | bytes 18436
  197.5 576.5 %copy-start.189 = (f32[2,768]{1,0:T(2,128)}, f32[2,768]{1,0:T(2,128)S(1)}, u32[]{:S(2)}) copy-start(f32[2,768]{1,0:T(2,128)S(1)} %get-tuple-element.280) | copy-start | bytes 18436
  197.5 578.7 %copy-start.185 = (f32[2,768]{1,0:T(2,128)}, f32[2,768]{1,0:T(2,128)S(1)}, u32[]{:S(2)}) copy-start(f32[2,768]{1,0:T(2,128)S(1)} %get-tuple-element.284) | copy-start | bytes 18436
  1054.9 269.2 %reduce-scatter.9.cloned.1.call-start = ((), (), s32[]{:S(2)}) async-start(), calls=%async_computation.8 | async-start | bytes 4866048 | tf_op jit(solution)/shard_map/reduce_scatter | solution.py:432
  1062.8 429.3 %reduce-scatter.7.cloned.1.call-start = ((), (), s32[]{:S(2)}) async-start(), calls=%async_computation.7 | async-start | bytes 14598144 | tf_op jit(solution)/shard_map/reduce_scatter | solution.py:431
  1090.8 611.7 %reduce-scatter.11.cloned.1.call-start = ((), (), s32[]{:S(2)}) async-start(), calls=%async_computation.9 | async-start | bytes 19464192 | tf_op jit(solution)/shard_map/reduce_scatter | solution.py:433
  1113.4 799.5 %reduce-scatter.13.cloned.1.call-start = ((), (), s32[]{:S(2)}) async-start(), calls=%async_computation.10 | async-start | bytes 19464192 | tf_op jit(solution)/shard_map/reduce_scatter | solution.py:434
  1162.1 1075.0 %reduce-scatter.15.cloned.1.call-start = ((), (), s32[]{:S(2)}) async-start(), calls=%async_computation.11 | async-start | bytes 34062336 | tf_op jit(solution)/shard_map/reduce_scatter | solution.py:435
  1325.7 958.3 %copy-start.154 = (f32[2056,24]{0,1:T(8,128)S(1)}, f32[2056,24]{0,1:T(8,128)}, u32[]{:S(2)}) copy-start(f32[2056,24]{0,1:T(8,128)} %param.40) | copy-start | bytes 592132
  (300 other events, 4457.9 us)
Sparse Core Ops, SparseCore 0:
  11.4 62.4 all-gather.18
  77.4 111.9 all-gather.20
  192.9 58.2 all-gather.22
  254.5 52.7 all-gather.24
  310.6 62.4 all-gather.26
  376.4 61.9 all-gather.28
  441.8 58.2 all-gather.30
  503.6 52.7 all-gather.32
  559.8 62.4 all-gather.34
  625.7 61.9 all-gather.36
  1055.0 155.9 all-reduce.5
  1216.3 107.8 reduce-scatter.8
  1330.1 161.8 reduce-scatter.6
  1498.3 204.1 reduce-scatter.10
  1708.8 204.1 reduce-scatter.12
  1919.2 317.8 reduce-scatter.14
where the time goes:
time: 2310 us; the launch traced here: 2300 us
  waiting for transfers between devices  1570 us (68%)
  matrix products  363 us (16%)
  other arithmetic  163 us (7%)
  local copies, waits for them, and re-layouts  138 us (6%)
  blocking collectives  39.8 us (2%)
  between operations  26.8 us (1%)
    reduce_scatter x1, waiting for transfers between devices, body(): lax.psum_scatter(grad_mod, 'fsdp', scatter_dimension=0, tiled=True)  322 us
    reduce_scatter x1, waiting for transfers between devices, body(): lax.psum_scatter(jnp.stack(grad_down), 'fsdp', scatter_dimension=1, tiled...  208 us
    reduce_scatter x1, waiting for transfers between devices, body(): lax.psum_scatter(jnp.stack(grad_up), 'fsdp', scatter_dimension=1, tiled=T...  207 us
    reduce_scatter x1, waiting for transfers between devices, body(): lax.psum_scatter(jnp.stack(grad_qkv), 'fsdp', scatter_dimension=1, tiled=...  166 us
    all_gather x2, waiting for transfers between devices, body(): lax.all_gather(up_low[layer_index], 'fsdp', axis=0, tiled=True)  122 us
    all_gather x2, waiting for transfers between devices, body(): lax.all_gather(down_low[layer_index], 'fsdp', axis=0, tiled=True)  117 us
    dot_general x26, matrix products, left_product(): lax.dot_general(left_side, right_side, (((0,), (0,)), ((), ())), preferre...  115 us
    reduce_scatter x1, waiting for transfers between devices, body(): lax.psum_scatter(jnp.stack(grad_proj), 'fsdp', scatter_dimension=1, tiled...  109 us
  transfers between devices with their start and end apart: 16, of which 16 were waited for; matrix products, arithmetic and copies ran while one was open for 12% of the time, Pallas kernels for 0%

commit v1 on v0

v1 whole, which is shorter than its diff:
```python
import math

import jax
import jax.numpy as jnp
from jax import lax
from jax.experimental import pallas as pl
from jax.sharding import PartitionSpec as P

D = 768
HEADS = 12
HD = 64
FF = 3072
FREQ = 256
CLASSES = 1000
DIFF_STEPS = 1000
LAYERS = 2
TOK = 256
PD = 16
MODW = 10752


norm_eps = 1e-06
clip_limit = 2.5
learn_rate = 0.01
beta_first = 0.9
beta_second = 0.95
adam_eps = 1e-08
weight_decay = 0.01
first_fix = 1.0 - 0.9**10
second_fix = 1.0 - 0.95**10


def modulate(residual, shift_term, scale_term):
    centred = residual - jnp.mean(residual, axis=-1, keepdims=True)
    spread = jnp.mean(centred * centred, axis=-1, keepdims=True)
    normed = centred * lax.rsqrt(spread + norm_eps)
    return normed * (1.0 + scale_term[:, None, :]) + shift_term[:, None, :]


def gelu_tanh(values):
    return jax.nn.gelu(values, approximate=True)


def product(left_side, right_side):
    return jnp.dot(left_side, right_side, preferred_element_type=jnp.float32)


def left_product(left_side, right_side):
    return lax.dot_general(
        left_side, right_side, (((0,), (0,)), ((), ())), preferred_element_type=jnp.float32
    )


def right_product(left_side, right_side):
    return lax.dot_general(
        left_side, right_side, (((1,), (1,)), ((), ())), preferred_element_type=jnp.float32
    )


def time_features(steps_in):
    half_count = FREQ // 2
    frequencies = jnp.exp(
        -math.log(10000.0) * jnp.arange(half_count, dtype=jnp.float32) / half_count
    )
    angles = steps_in.astype(jnp.float32)[:, None] * frequencies[None, :]
    return jnp.concatenate([jnp.cos(angles), jnp.sin(angles)], axis=1)


def noise_share(steps_in):
    beta_values = jnp.linspace(0.0001, 0.02, DIFF_STEPS, dtype=jnp.float32)
    log_keep = jnp.log(1.0 - beta_values)
    taken = jnp.arange(DIFF_STEPS, dtype=jnp.int32)[None, :] <= steps_in[:, None]
    return jnp.exp(jnp.sum(jnp.where(taken, log_keep[None, :], 0.0), axis=1))


def bias_parts(biases):
    per_layer = 10 * D + FF
    layer_parts = []
    for layer_index in range(LAYERS):
        anchor = layer_index * per_layer
        layer_parts.append(
            (
                biases[anchor : anchor + D],
                biases[anchor + D : anchor + 2 * D],
                biases[anchor + 2 * D : anchor + 3 * D],
                biases[anchor + 3 * D : anchor + 3 * D + FF],
                biases[anchor + 3 * D + FF : anchor + 4 * D + FF],
                biases[anchor + 4 * D + FF : anchor + per_layer],
            )
        )
    anchor = LAYERS * per_layer
    global_parts = (
        biases[anchor : anchor + 2 * D],
        biases[anchor + 2 * D : anchor + 3 * D],
        biases[anchor + 3 * D : anchor + 4 * D],
        biases[anchor + 4 * D : anchor + 5 * D],
        biases[anchor + 5 * D : anchor + 5 * D + PD],
    )
    return (layer_parts, global_parts)


def hop_plan(count):
    if count == 32:
        return [(8, 4), (2, 2), (4, 2), (1, 2)]
    plan = []
    stride = 1
    while stride < count:
        plan.append((stride, 2))
        stride *= 2
    return plan


def shifted(index, stride, size, amount):
    coord = (index // stride) % size
    return index + ((coord + amount) % size - coord) * stride


def send(value, count, stride, size, amount=1):
    pairs = [(index, shifted(index, stride, size, amount)) for index in range(count)]
    return lax.ppermute(value, "fsdp", pairs)


def gather_near(value, count):
    gathered = value[None]
    for stride, size in hop_plan(count):
        pieces = [gathered]
        for unused in range(size - 1):
            pieces.append(send(pieces[-1], count, stride, size))
        gathered = jnp.concatenate(pieces, axis=0)
    return gathered


def near_places(count):
    me = lax.axis_index("fsdp")
    others = jnp.arange(count, dtype=jnp.int32)
    places = jnp.zeros((count,), jnp.int32)
    weight = 1
    for stride, size in hop_plan(count):
        steps = ((me // stride) % size - (others // stride) % size) % size
        places = places + steps * weight
        weight *= size
    return places


def mesh_dims(count):
    if count == 32:
        return (4, 2, 2, 2)
    return (2,) * (count.bit_length() - 1)


def fold(parts, axis, stride, count):
    size = parts[0].shape[axis]
    mine = (lax.axis_index("fsdp") // stride) % size

    def entry(index):
        picked = [lax.dynamic_index_in_dim(part, index, axis, keepdims=False) for part in parts]
        return picked[0] if len(picked) == 1 else jnp.concatenate(picked, axis=-2)

    arrived = [
        send(entry((mine + step) % size), count, stride, size, step) for step in range(1, size)
    ]
    total = entry(mine).astype(jnp.float32)
    for piece in arrived:
        total = total + piece.astype(jnp.float32)
    return total


def scatter_sum(parts, count):
    dims = mesh_dims(count)
    strides = [1]
    for size in reversed(dims[1:]):
        strides.insert(0, strides[0] * size)
    last = len(dims) - 1
    shaped = [part.reshape(dims + part.shape[1:]) for part in parts]
    paired = fold(shaped, last, strides[last], count).astype(jnp.bfloat16)
    half = paired.shape[-2] // 2
    results = []
    for lane, order in enumerate((range(last - 1, -1, -1), range(last - 1, -1, -1))):
        axes = list(range(last))
        chosen_axes = list(order)
        if lane == 1 and last >= 2:
            chosen_axes[0], chosen_axes[1] = chosen_axes[1], chosen_axes[0]
        value = paired[..., :half, :] if lane == 0 else paired[..., half:, :]
        for step, axis in enumerate(chosen_axes):
            place = axes.index(axis)
            value = fold([value], place, strides[axis], count)
            axes.remove(axis)
            if step + 1 < last:
                value = value.astype(jnp.bfloat16)
        results.append(value)
    return jnp.concatenate(results, axis=0)


def sum_all(value, count):
    stride = 1
    while stride < count:
        value = value + send(value, count, stride, 2)
        stride *= 2
    return value


def pair_scores(queries, keys_all, first_half):
    only = jnp.where(first_half, queries, jnp.zeros_like(queries))
    return only, right_product(only, keys_all) * HD ** (-0.5)


def attention_forward_kernel(queries_ref, keys_ref, values_ref, mixed_ref, total_ref):
    lanes = lax.broadcasted_iota(jnp.int32, (TOK, 2 * HD), 1)
    totals = jnp.zeros((TOK, 2 * HD), jnp.float32)
    for pair in range(HEADS // 2):
        span = slice(pair * 2 * HD, (pair + 1) * 2 * HD)
        queries, keys_all, values_all = queries_ref[:, span], keys_ref[:, span], values_ref[:, span]
        halves = []
        for half in range(2):
            mine = (lanes < HD) if half == 0 else (lanes >= HD)
            unused, scores = pair_scores(queries, keys_all, mine)
            row_max = jnp.max(scores, axis=1, keepdims=True)
            raised = jnp.exp(scores - row_max)
            row_sum = jnp.sum(raised, axis=1, keepdims=True)
            soft_low = (raised / row_sum).astype(jnp.bfloat16)
            halves.append(product(soft_low, values_all))
            totals = jnp.where(lanes == 2 * pair + half, row_max + jnp.log(row_sum), totals)
        mixed_ref[:, span] = jnp.where(lanes < HD, halves[0], halves[1]).astype(jnp.bfloat16)
    total_ref[...] = totals


def attention_backward_kernel(
    queries_ref, keys_ref, values_ref, total_ref, grad_ref, dqueries_ref, dkeys_ref, dvalues_ref
):
    lanes = lax.broadcasted_iota(jnp.int32, (TOK, 2 * HD), 1)
    for pair in range(HEADS // 2):
        span = slice(pair * 2 * HD, (pair + 1) * 2 * HD)
        queries, keys_all, values_all = queries_ref[:, span], keys_ref[:, span], values_ref[:, span]
        grads = grad_ref[:, span]
        made = []
        for half in range(2):
            mine = (lanes < HD) if half == 0 else (lanes >= HD)
            unused, scores = pair_scores(queries, keys_all, mine)
            head = 2 * pair + half
            soft_weights = jnp.exp(scores - total_ref[:, head : head + 1])
            grad_values = left_product(soft_weights.astype(jnp.bfloat16), grads)
            grad_soft = right_product(jnp.where(mine, grads, jnp.zeros_like(grads)), values_all)
            spread = jnp.sum(soft_weights * grad_soft, axis=1, keepdims=True)
            score_low = (soft_weights * (grad_soft - spread)).astype(jnp.bfloat16)
            made.append(
                (
                    product(score_low, keys_all) * HD ** (-0.5),
                    left_product(score_low, queries) * HD ** (-0.5),
                    grad_values,
                )
            )
        for part, target in enumerate((dqueries_ref, dkeys_ref, dvalues_ref)):
            target[:, span] = jnp.where(lanes < HD, made[0][part], made[1][part]).astype(
                jnp.bfloat16
            )


def token_block(width):
    return pl.BlockSpec((TOK, width), lambda sample: (sample, 0))


def attention_forward(packed_low, sample_count):
    row_count = sample_count * TOK
    return pl.pallas_call(
        attention_forward_kernel,
        grid=(sample_count,),
        in_specs=[token_block(D)] * 3,
        out_specs=[token_block(D), token_block(2 * HD)],
        out_shape=[
            jax.ShapeDtypeStruct((row_count, D), jnp.bfloat16),
            jax.ShapeDtypeStruct((row_count, 2 * HD), jnp.float32),
        ],
        name="attention_forward",
    )(*packed_low)


def attention_backward(packed_low, log_total, grad_mixed_low, sample_count):
    row_count = sample_count * TOK
    return pl.pallas_call(
        attention_backward_kernel,
        grid=(sample_count,),
        in_specs=[token_block(D)] * 3 + [token_block(2 * HD), token_block(D)],
        out_specs=[token_block(D)] * 3,
        out_shape=[jax.ShapeDtypeStruct((row_count, D), jnp.bfloat16)] * 3,
        name="attention_backward",
    )(*packed_low, log_total, grad_mixed_low)


def adam_step(weight_now, grad_now, first_old, second_old, factor):
    clipped = grad_now * factor
    first_new = beta_first * first_old + (1.0 - beta_first) * clipped
    second_new = beta_second * second_old + (1.0 - beta_second) * clipped * clipped
    step_size = -learn_rate * (
        first_new / first_fix / (jnp.sqrt(second_new / second_fix) + adam_eps)
        + weight_decay * weight_now
    )
    return (step_size, first_new, second_new)


def body(
    latents,
    noise,
    timesteps,
    labels,
    qkv_weight,
    proj_weight,
    up_weight,
    down_weight,
    mod_weight,
    tables,
    biases,
    qkv_first,
    proj_first,
    up_first,
    down_first,
    mod_first,
    tables_first,
    biases_first,
    qkv_second,
    proj_second,
    up_second,
    down_second,
    mod_second,
    tables_second,
    biases_second,
):
    count = lax.axis_size("fsdp")
    me = lax.axis_index("fsdp")
    local = latents.shape[0]
    samples = local * count
    rows = D // count
    row_count = local * TOK
    total_count = samples * TOK * PD
    low = jnp.bfloat16
    f32 = jnp.float32
    layer_parts, global_parts = bias_parts(biases)
    final_bias, patch_bias, first_bias, second_bias, head_bias = global_parts
    mod_bias = jnp.concatenate([part_item[5] for part_item in layer_parts] + [final_bias])

    gathered = []
    for layer_index in range(LAYERS):
        pieces = [qkv_weight[layer_index][:, part * D : (part + 1) * D] for part in range(3)]
        pieces.append(proj_weight[layer_index])
        pieces += [up_weight[layer_index][:, part * D : (part + 1) * D] for part in range(4)]
        pieces.append(down_weight[layer_index])
        packed = jnp.concatenate(pieces, axis=0).astype(low)
        gathered.append(
            lax.all_gather(packed, "fsdp", axis=0, tiled=True).reshape(count, 12 * rows, D)
        )

    mod_low = mod_weight.astype(low)
    mod_columns = lax.all_to_all(mod_low, "fsdp", split_axis=1, concat_axis=0, tiled=True)
    digits = jnp.concatenate([timesteps // 32, timesteps % 32, labels // 32, labels % 32]).astype(low)
    table_low = tables.astype(low).T
    room = -(-CLASSES // 128) * 128
    first_at, class_at, patch_at = D, D + FREQ, D + FREQ + room
    head_at, digit_at = patch_at + PD, patch_at + 2 * PD
    tables_low = jnp.concatenate(
        [
            table_low[:, PD + FREQ : PD + FREQ + D],
            table_low[:, PD : PD + FREQ],
            table_low[:, PD + FREQ + D : PD + FREQ + D + CLASSES],
            jnp.zeros((rows, room - CLASSES), low),
            table_low[:, :PD],
            table_low[:, PD + FREQ + D + CLASSES :],
            jnp.broadcast_to(digits[None, :], (rows, 4 * local)),
        ],
        axis=1,
    )
    tables_near = gather_near(tables_low, count)
    places = near_places(count)
    tables_far = jnp.take(tables_near, places, axis=0, mode="clip")
    tables_full = tables_far.reshape(D, digit_at + 4 * local)
    second_near = tables_near[:, :, :D].reshape(D, D)

    def read_digits(from_devices):
        numbers = from_devices[:, 0, digit_at:].astype(jnp.int32).reshape(count, 4, local)
        steps_all = (numbers[:, 0] * 32 + numbers[:, 1]).reshape(samples)
        labels_all = (numbers[:, 2] * 32 + numbers[:, 3]).reshape(samples)
        return steps_all, labels_all

    def embed(steps_all):
        features_low = time_features(steps_all).astype(low)
        first_pre = right_product(features_low, tables_full[:, first_at:class_at]) + first_bias
        return features_low, first_pre, jax.nn.silu(first_pre).astype(low)

    def chosen(labels_all):
        return (labels_all[:, None] == jnp.arange(room, dtype=jnp.int32)[None, :]).astype(low)

    steps_far, labels_far = read_digits(tables_far)
    features_far, first_pre_far, first_low_far = embed(steps_far)
    condition_far = (
        right_product(first_low_far, tables_full[:, :D])
        + second_bias
        + right_product(chosen(labels_far), tables_full[:, class_at:patch_at])
    )
    mods_columns = product(jax.nn.silu(condition_far).astype(low), mod_columns)
    modulations = (
        lax.all_to_all(mods_columns, "fsdp", split_axis=0, concat_axis=1, tiled=True) + mod_bias
    )

    keep_share = noise_share(timesteps)
    noised = (
        jnp.sqrt(keep_share)[:, None, None] * latents
        + jnp.sqrt(1.0 - keep_share)[:, None, None] * noise
    )
    noised_low = noised.reshape(row_count, PD).astype(low)
    patch_columns = tables_full[:, patch_at:head_at]
    head_columns = tables_full[:, head_at:digit_at]
    residual = (right_product(noised_low, patch_columns) + patch_bias).reshape(local, TOK, D)

    def weights_of(layer_index):
        whole = gathered[layer_index]
        square = [
            whole[:, part * rows : (part + 1) * rows].reshape(D, D) for part in range(8)
        ]
        up_full = jnp.concatenate(square[4:], axis=1)
        down_full = whole[:, 8 * rows :].reshape(FF, D)
        return square[:3], square[3], up_full, down_full

    stored = []
    for layer_index in range(LAYERS):
        gathered[layer_index], residual = lax.optimization_barrier(
            (gathered[layer_index], residual)
        )
        qkv_full, proj_full, up_full, down_full = weights_of(layer_index)
        query_bias, value_bias, proj_bias, up_bias, down_bias, unused = layer_parts[layer_index]
        segment = modulations[:, layer_index * 6 * D : (layer_index + 1) * 6 * D]
        mod_terms = [segment[:, part_index * D : (part_index + 1) * D] for part_index in range(6)]
        shift_attn, scale_attn, gate_attn, shift_mlp, scale_mlp, gate_mlp = mod_terms
        residual_in = residual
        hidden_low = modulate(residual_in, shift_attn, scale_attn).reshape(row_count, D).astype(low)
        packed_low = [
            (product(hidden_low, qkv_full[0]) + query_bias).astype(low),
            product(hidden_low, qkv_full[1]).astype(low),
            (product(hidden_low, qkv_full[2]) + value_bias).astype(low),
        ]
        mixed, log_total = attention_forward(packed_low, local)
        mixed_low = mixed.astype(low)
        attn_out = (product(mixed_low, proj_full) + proj_bias).reshape(local, TOK, D)
        residual_mid = residual_in + gate_attn[:, None, :] * attn_out
        hidden_two_low = modulate(residual_mid, shift_mlp, scale_mlp).reshape(row_count, D).astype(low)
        pre_act = product(hidden_two_low, up_full) + up_bias
        act_low = gelu_tanh(pre_act).astype(low)
        mlp_out = (product(act_low, down_full) + down_bias).reshape(local, TOK, D)
        residual = residual_mid + gate_mlp[:, None, :] * mlp_out
        stored.append(
            (
                residual_in,
                hidden_low,
                packed_low,
                log_total,
                mixed_low,
                attn_out,
                residual_mid,
                hidden_two_low,
                pre_act,
                act_low,
                mlp_out,
            )
        )
    final_mods = modulations[:, LAYERS * 6 * D :]
    final_hidden = modulate(residual, final_mods[:, :D], final_mods[:, D:])
    final_low = final_hidden.reshape(row_count, D).astype(low)
    predicted = product(final_low, head_columns) + head_bias
    errors = predicted - noise.reshape(row_count, PD)
    loss_local = jnp.sum(errors * errors) / total_count
    grad_pred_low = (2.0 * errors / total_count).astype(low)
    grad_head_bias = jnp.sum(grad_pred_low.astype(f32), axis=0)
    grad_head = left_product(grad_pred_low, final_low)
    grad_final = right_product(grad_pred_low, head_columns).reshape(local, TOK, D)
    unused, final_pull = jax.vjp(modulate, residual, final_mods[:, :D], final_mods[:, D:])
    grad_residual, grad_shift_final, grad_scale_final = final_pull(grad_final)
    mod_grads = [None] * LAYERS
    shards = [None] * LAYERS
    bias_pieces = [None] * LAYERS
    for layer_index in reversed(range(LAYERS)):
        qkv_full, proj_full, up_full, down_full = weights_of(layer_index)
        (
            residual_in,
            hidden_low,
            packed_low,
            log_total,
            mixed_low,
            attn_out,
            residual_mid,
            hidden_two_low,
            pre_act,
            act_low,
            mlp_out,
        ) = stored[layer_index]
        segment = modulations[:, layer_index * 6 * D : (layer_index + 1) * 6 * D]
        mod_terms = [segment[:, part_index * D : (part_index + 1) * D] for part_index in range(6)]
        shift_attn, scale_attn, gate_attn, shift_mlp, scale_mlp, gate_mlp = mod_terms
        grad_gate_mlp = jnp.sum(grad_residual * mlp_out, axis=1)
        grad_mlp_low = (grad_residual * gate_mlp[:, None, :]).reshape(row_count, D).astype(low)
        grad_down_bias = jnp.sum(grad_mlp_low.astype(f32), axis=0)
        grad_down = left_product(act_low, grad_mlp_low)
        grad_act = right_product(grad_mlp_low, down_full)
        unused, gelu_pull = jax.vjp(gelu_tanh, pre_act)
        grad_pre_low = gelu_pull(grad_act)[0].astype(low)
        grad_up_bias = jnp.sum(grad_pre_low.astype(f32), axis=0)
        grad_up = left_product(hidden_two_low, grad_pre_low)
        grad_hidden_two = right_product(grad_pre_low, up_full).reshape(local, TOK, D)
        unused, mlp_pull = jax.vjp(modulate, residual_mid, shift_mlp, scale_mlp)
        part_residual, grad_shift_mlp, grad_scale_mlp = mlp_pull(grad_hidden_two)
        grad_residual = grad_residual + part_residual
        grad_gate_attn = jnp.sum(grad_residual * attn_out, axis=1)
        grad_attn_low = (grad_residual * gate_attn[:, None, :]).reshape(row_count, D).astype(low)
        grad_proj_bias = jnp.sum(grad_attn_low.astype(f32), axis=0)
        grad_proj = left_product(mixed_low, grad_attn_low)
        grad_mixed_low = right_product(grad_attn_low, proj_full).astype(low)
        grad_packed_low = attention_backward(packed_low, log_total, grad_mixed_low, local)
        grad_query_bias = jnp.sum(grad_packed_low[0].astype(f32), axis=0)
        grad_value_bias = jnp.sum(grad_packed_low[2].astype(f32), axis=0)
        grad_qkv = [left_product(hidden_low, item) for item in grad_packed_low]
        grad_hidden = (
            right_product(grad_packed_low[0], qkv_full[0])
            + right_product(grad_packed_low[1], qkv_full[1])
            + right_product(grad_packed_low[2], qkv_full[2])
        ).reshape(local, TOK, D)
        unused, attn_pull = jax.vjp(modulate, residual_in, shift_attn, scale_attn)
        part_residual, grad_shift_attn, grad_scale_attn = attn_pull(grad_hidden)
        grad_residual = grad_residual + part_residual
        mod_grads[layer_index] = jnp.concatenate(
            [
                grad_shift_attn,
                grad_scale_attn,
                grad_gate_attn,
                grad_shift_mlp,
                grad_scale_mlp,
                grad_gate_mlp,
            ],
            axis=1,
        )
        sent = [item.astype(low).reshape(count, rows, D) for item in grad_qkv + [grad_proj]]
        sent += [
            grad_up[:, part * D : (part + 1) * D].astype(low).reshape(count, rows, D)
            for part in range(4)
        ]
        sent.append(grad_down.astype(low).reshape(count, 4 * rows, D))
        if layer_index > 0:
            sent = jnp.concatenate(sent, axis=1).reshape(count * 12 * rows, D)
            sent, grad_residual = lax.optimization_barrier((sent, grad_residual))
            shard = lax.psum_scatter(sent, "fsdp", scatter_dimension=0, tiled=True).astype(f32)
        else:
            shard = scatter_sum(sent, count)
        parts = [shard[part * rows : (part + 1) * rows] for part in range(8)]
        shards[layer_index] = (
            jnp.concatenate(parts[:3], axis=1),
            parts[3],
            jnp.concatenate(parts[4:], axis=1),
            shard[8 * rows :],
        )
        bias_pieces[layer_index] = [
            grad_query_bias,
            grad_value_bias,
            grad_proj_bias,
            grad_up_bias,
            grad_down_bias,
        ]
    grad_zero_low = grad_residual.reshape(row_count, D).astype(low)
    grad_patch_bias = jnp.sum(grad_zero_low.astype(f32), axis=0)
    grad_patch = left_product(noised_low, grad_zero_low)

    grad_mods_low = jnp.concatenate(mod_grads + [grad_shift_final, grad_scale_final], axis=1)
    grad_mods_near = gather_near(grad_mods_low.astype(low), count).reshape(samples, MODW)
    steps_near, labels_near = read_digits(tables_near)
    unused, unused_pre, first_low = embed(steps_near)
    class_near = chosen(labels_near)
    own_second = tables_low[:, :D]
    own_class = tables_low[:, class_at:patch_at]
    own_bias = lax.dynamic_slice(second_bias, (me * rows,), (rows,))
    condition = (
        right_product(first_low, own_second) + own_bias + right_product(class_near, own_class)
    )
    condition_act, silu_pull = jax.vjp(jax.nn.silu, condition)
    shard_mod = left_product(condition_act.astype(low), grad_mods_near)
    grad_mod_bias = jnp.sum(grad_mods_near.astype(f32), axis=0)
    grad_condition = silu_pull(right_product(grad_mods_near, mod_low))[0]
    grad_class = lax.dot_general(
        class_near.astype(f32),
        grad_condition,
        (((0,), (0,)), ((), ())),
        precision=lax.Precision.HIGHEST,
        preferred_element_type=f32,
    )[:CLASSES]
    grad_time_low = grad_condition.astype(low)
    grad_second_bias = jnp.sum(grad_time_low.astype(f32), axis=0)
    grad_second = left_product(first_low, grad_time_low)
    far_order = (places[:, None] * local + jnp.arange(local, dtype=jnp.int32)[None, :]).reshape(-1)
    reorder = (jnp.arange(samples, dtype=jnp.int32)[:, None] == far_order[None, :]).astype(low)
    grad_time_far = left_product(grad_time_low, reorder).astype(low)
    grad_time_near = gather_near(grad_time_far, count).reshape(D, samples)
    grad_first_act = left_product(grad_time_near, second_near)
    unused, first_pull = jax.vjp(jax.nn.silu, first_pre_far)
    grad_first_low = first_pull(grad_first_act)[0].astype(low)
    grad_first_low = lax.dynamic_slice(grad_first_low, (0, me * rows), (samples, rows))
    grad_first_bias = jnp.sum(grad_first_low.astype(f32), axis=0)
    grad_first = left_product(features_far, grad_first_low)

    def spread(piece, length):
        return lax.dynamic_update_slice(jnp.zeros((length,), f32), piece, (me * piece.shape[0],))

    columns = MODW // count
    own_mod_bias = spread(lax.dynamic_slice(grad_mod_bias, (me * columns,), (columns,)), MODW)
    pieces = []
    for layer_index in range(LAYERS):
        pieces += bias_pieces[layer_index]
        pieces.append(own_mod_bias[layer_index * 6 * D : (layer_index + 1) * 6 * D])
    pieces += [
        own_mod_bias[LAYERS * 6 * D :],
        grad_patch_bias,
        spread(grad_first_bias, D),
        spread(grad_second_bias, D),
        grad_head_bias,
    ]
    ends = sum_all(jnp.concatenate([grad_patch, grad_head], axis=0), count)
    own_ends = lax.dynamic_slice(ends, (0, me * rows), (2 * PD, rows))
    shard_tables = jnp.concatenate(
        [own_ends[:PD], grad_first, grad_second, grad_class, own_ends[PD:]], axis=0
    )
    shard_squares = jnp.sum(shard_mod * shard_mod) + jnp.sum(shard_tables * shard_tables)
    for layer_index in range(LAYERS):
        for item in shards[layer_index]:
            shard_squares = shard_squares + jnp.sum(item * item)
    bias_length = biases.shape[0]
    pieces += [shard_squares[None], loss_local[None]]
    summed = sum_all(jnp.concatenate(pieces), count)
    bias_grad = summed[:bias_length]
    square_total = summed[bias_length]
    loss_value = summed[bias_length + 1]
    grad_norm = jnp.sqrt(square_total + jnp.sum(bias_grad * bias_grad))
    factor = jnp.minimum(1.0, clip_limit / (grad_norm + 1e-06))
    shard_qkv, shard_proj, shard_up, shard_down = [
        jnp.stack([shards[layer_index][part] for layer_index in range(LAYERS)]) for part in range(4)
    ]
    qkv_update, qkv_first_new, qkv_second_new = adam_step(
        qkv_weight, shard_qkv, qkv_first, qkv_second, factor
    )
    proj_update, proj_first_new, proj_second_new = adam_step(
        proj_weight, shard_proj, proj_first, proj_second, factor
    )
    up_update, up_first_new, up_second_new = adam_step(
        up_weight, shard_up, up_first, up_second, factor
    )
    down_update, down_first_new, down_second_new = adam_step(
        down_weight, shard_down, down_first, down_second, factor
    )
    mod_update, mod_first_new, mod_second_new = adam_step(
        mod_weight, shard_mod, mod_first, mod_second, factor
    )
    tables_update, tables_first_new, tables_second_new = adam_step(
        tables, shard_tables, tables_first, tables_second, factor
    )
    biases_update, biases_first_new, biases_second_new = adam_step(
        biases, bias_grad, biases_first, biases_second, factor
    )
    return (
        loss_value,
        grad_norm,
        qkv_update,
        qkv_first_new,
        qkv_second_new,
        proj_update,
        proj_first_new,
        proj_second_new,
        up_update,
        up_first_new,
        up_second_new,
        down_update,
        down_first_new,
        down_second_new,
        mod_update,
        mod_first_new,
        mod_second_new,
        tables_update,
        tables_first_new,
        tables_second_new,
        biases_update,
        biases_first_new,
        biases_second_new,
    )


def solution(mesh):
    in_specs = (
        P("fsdp", None, None),
        P("fsdp", None, None),
        P("fsdp"),
        P("fsdp"),
        P(None, "fsdp", None),
        P(None, "fsdp", None),
        P(None, "fsdp", None),
        P(None, "fsdp", None),
        P("fsdp", None),
        P(None, "fsdp"),
        P(),
        P(None, "fsdp", None),
        P(None, "fsdp", None),
        P(None, "fsdp", None),
        P(None, "fsdp", None),
        P("fsdp", None),
        P(None, "fsdp"),
        P(),
        P(None, "fsdp", None),
        P(None, "fsdp", None),
        P(None, "fsdp", None),
        P(None, "fsdp", None),
        P("fsdp", None),
        P(None, "fsdp"),
        P(),
    )
    out_specs = (
        P(),
        P(),
        P(None, "fsdp", None),
        P(None, "fsdp", None),
        P(None, "fsdp", None),
        P(None, "fsdp", None),
        P(None, "fsdp", None),
        P(None, "fsdp", None),
        P(None, "fsdp", None),
        P(None, "fsdp", None),
        P(None, "fsdp", None),
        P(None, "fsdp", None),
        P(None, "fsdp", None),
        P(None, "fsdp", None),
        P("fsdp", None),
        P("fsdp", None),
        P("fsdp", None),
        P(None, "fsdp"),
        P(None, "fsdp"),
        P(None, "fsdp"),
        P(),
        P(),
        P(),
    )
    return jax.shard_map(body, mesh=mesh, in_specs=in_specs, out_specs=out_specs, check_vma=False)
```

time: 2310 us -> 904 us (0.39)
  waiting for transfers between devices: 1570 us -> 259 us
  matrix products: 363 us -> 209 us
  Pallas kernels: 0 us -> 68.7 us
  other arithmetic: 163 us -> 116 us
  starting transfers between devices: 1.69 us -> 42.4 us
  blocking collectives: 39.8 us -> 0 us
  local copies, waits for them, and re-layouts: 138 us -> 171 us
    reduce_scatter x5 -> x1, waiting for transfers between devices: 1010 us -> 0.02 us  [body(): lax.psum_scatter(sent, 'fsdp', scatter_dimension=0, tiled=True).astype(f32)]
    all_gather x10 -> x2, waiting for transfers between devices: 548 us -> 55.7 us  [body(): lax.all_gather(packed, 'fsdp', axis=0, tiled=True)]
    ppermute x0 -> x39, waiting for transfers between devices: none -> 195 us  [send(): return lax.ppermute(value, 'fsdp', pairs)]
    pallas_call x0 -> x4, Pallas kernels: none -> 68.7 us  [the longest x2 47.7 us: attention_backward(): pl.pallas_call(attention_backward_kernel, grid=(sample_count,), in_specs=...]
    dot_general x24 -> x1, matrix products: 57.2 us -> 0.92 us  [body(): lax.dot_general(class_near.astype(f32), grad_condition, (((0,), (0,)), ((...]
    dot_general x26 -> x19, matrix products: 115 us -> 68.1 us  [left_product(): lax.dot_general(left_side, right_side, (((0,), (0,)), ((), ())), preferre...]
    concatenate x4 -> x15, local copies, waits for them, and re-layouts: 0.21 us -> 44.9 us  [the longest x8 36.2 us: gather_near(): gathered = jnp.concatenate(pieces, axis=0)]
    psum x1 -> x0, blocking collectives: 39.8 us -> none  [body(): lax.psum((bias_local, shard_squares, loss_local), 'fsdp')]
  transfers between devices with their start and end apart: 16 -> 44, of which waited for: 16 -> 29; matrix products, arithmetic and copies ran while one was open for 12% -> 26% of each run, Pallas kernels for 0% -> 1%
where the time goes in v1:
time: 904 us; the launch traced here: 893 us
  waiting for transfers between devices  259 us (29%)
  matrix products  209 us (23%)
  local copies, waits for them, and re-layouts  171 us (19%)
  other arithmetic  116 us (13%)
  Pallas kernels  68.7 us (8%)
  starting transfers between devices  42.4 us (5%)
  between operations  26.7 us (3%)
    ppermute x39, waiting for transfers between devices, send(): return lax.ppermute(value, 'fsdp', pairs)  195 us
    dot_general x21, matrix products, right_product(): lax.dot_general(left_side, right_side, (((1,), (1,)), ((), ())), preferre...  76.1 us
    dot_general x19, matrix products, left_product(): lax.dot_general(left_side, right_side, (((0,), (0,)), ((), ())), preferre...  68.1 us
    dot_general x14, matrix products, product(): return jnp.dot(left_side, right_side, preferred_element_type=jnp.float32)  63.6 us
    unnamed x460, local copies, waits for them, and re-layouts  57.9 us
    all_gather x2, waiting for transfers between devices, body(): lax.all_gather(packed, 'fsdp', axis=0, tiled=True)  55.7 us
    pallas_call x2, Pallas kernels, attention_backward(): pl.pallas_call(attention_backward_kernel, grid=(sample_count,), in_specs=...  47.7 us
    concatenate x8, local copies, waits for them, and re-layouts, gather_near(): gathered = jnp.concatenate(pieces, axis=0)  36.2 us
  transfers between devices with their start and end apart: 44, of which 29 were waited for; matrix products, arithmetic and copies ran while one was open for 26% of the time, Pallas kernels for 1%

profile of v1, /device:TPU:0, one launch (start us, length us, event | category | flops | bytes accessed | tf_op | source)
XLA Modules:
  0.0 892.6 jit_solution(16701787607793422851)
XLA Ops:
  59.8 14.9 %collective-permute-done.4 = bf16[8,24,2096]{2,1,0:T(8,128)(2,1)} collective-permute-done((bf16[8,24,2096]{2,1,0:T(8,128)(2,1)}, bf16[8,24,2096]{2,1,0:T(8,128)(2,1)}, u32[]{:S(2)}, u32[]{:S(2)}) %collective-permute-start.4) | collective-permute-done | bytes 804896 | tf_op jit(solution)/shard_map/ppermute | solution.py:120
  119.4 13.4 %all-gather.3.cloned.1.call-done = bf16[9216,768]{1,0:T(8,128)(2,1)} async-done(((bf16[288,768]{1,0:T(8,128)(2,1)}), bf16[9216,768]{1,0:T(8,128)(2,1)}) %all-gather.3.cloned.1.call-update) | async-done | bytes 14155792 | tf_op jit(solution)/shard_map/all_gather | solution.py:348
  155.0 10.3 %attention_forward.2 = (bf16[1024,768]{1,0:T(8,128)(2,1)}, f32[1024,128]{1,0:T(8,128)}) custom-call(bf16[1024,768]{1,0:T(8,128)(2,1)} %add_convert_fusion.9.queries_ref, bf16[1024,768]{1,0:T(8,128)(2,1)} %convolution_convert_fusion.7.keys_ref, bf16[1024,768]{1,0:T(8,128)(2,1)} %add_convert_fusion.8.values_ref), custom_call_target="tpu_custom_call" | custom-call | tf_op jit(solution)/shard_map/attention_forward/pallas_call | solution.py:264
  174.2 8.3 fusion.34
  182.5 10.9 %convolution_add_fusion.4 = f32[1024,768]{1,0:T(8,128)S(1)} fusion(bf16[3072,768]{1,0:T(8,128)(2,1)S(1)} %bitcast.409, f32[768]{0:T(1024)S(1)} %copy-done.171, f32[1024,3072]{1,0:T(8,128)} %fusion.34, f32[3072]{0:T(1024)S(1)} %copy-done.162), kind=kOutput, calls=%fused_computation.114 | convolution fusion | flops 4864081920 | bytes 20462592 | tf_op jit(solution)/shard_map/dot_general | solution.py:45
  195.8 42.4 %all-gather.5.cloned.1.call-done = bf16[9216,768]{1,0:T(8,128)(2,1)} async-done(((bf16[288,768]{1,0:T(8,128)(2,1)}), bf16[9216,768]{1,0:T(8,128)(2,1)}) %all-gather.5.cloned.1.call-update) | async-done | bytes 14155792 | tf_op jit(solution)/shard_map/all_gather | solution.py:348
  259.6 10.7 %attention_forward.3 = (bf16[1024,768]{1,0:T(8,128)(2,1)}, f32[1024,128]{1,0:T(8,128)}) custom-call(bf16[1024,768]{1,0:T(8,128)(2,1)} %add_convert_fusion.5.queries_ref, bf16[1024,768]{1,0:T(8,128)(2,1)} %convolution_convert_fusion.6.keys_ref, bf16[1024,768]{1,0:T(8,128)(2,1)} %add_convert_fusion.4.values_ref), custom_call_target="tpu_custom_call" | custom-call | tf_op jit(solution)/shard_map/attention_forward/pallas_call | solution.py:264
  279.3 8.3 fusion.32
  287.6 10.7 %convolution_add_fusion.3 = f32[1024,768]{1,0:T(8,128)S(1)} fusion(bf16[3072,768]{1,0:T(8,128)(2,1)S(1)} %bitcast.421, f32[768]{0:T(1024)S(1)} %copy-done.167, f32[1024,3072]{1,0:T(8,128)} %fusion.32, f32[3072]{0:T(1024)S(1)} %copy-done.164), kind=kOutput, calls=%fused_computation.113 | convolution fusion | flops 4864081920 | bytes 20462592 | tf_op jit(solution)/shard_map/dot_general | solution.py:45
  316.3 15.6 %convert_reduce_fusion = (f32[3072]{0:T(1024)}, bf16[1024,3072]{1,0:T(8,128)(2,1)S(1)}) fusion(f32[1024,3072]{1,0:T(8,128)} %fusion.32, f32[3072]{0:T(1024)S(1)} %copy-done.164, bf16[1024,768]{1,0:T(8,128)(2,1)S(1)} %bitcast.447, bf16[3072,768]{1,0:T(8,128)(2,1)} %bitcast.418), kind=kOutput, calls=%fused_computation.20 | convolution fusion | flops 4904186880 | bytes 25190400 | tf_op jit(solution)/shard_map/dot_general | solution.py:55
  331.9 14.8 %convolution_convert_fusion.2 = bf16[3072,768]{1,0:T(8,128)(2,1)} fusion(bf16[1024,768]{1,0:T(8,128)(2,1)S(1)} %bitcast.448, f32[1024,3072]{1,0:T(8,128)} %fusion.32, f32[3072]{0:T(1024)S(1)} %copy-done.164), kind=kOutput, calls=%fused_computation.27 | convolution fusion | flops 4865654784 | bytes 18886656 | tf_op jit(solution)/shard_map/dot_general | solution.py:49
  365.9 23.9 %attention_backward.2 = (bf16[1024,768]{1,0:T(8,128)(2,1)}, bf16[1024,768]{1,0:T(8,128)(2,1)}, bf16[1024,768]{1,0:T(8,128)(2,1)}) custom-call(bf16[1024,768]{1,0:T(8,128)(2,1)} %add_convert_fusion.5.queries_ref, bf16[1024,768]{1,0:T(8,128)(2,1)} %convolution_convert_fusion.6.keys_ref, bf16[1024,768]{1,0:T(8,128)(2,1)} %add_convert_fusion.4.values_ref, ...), custom_call_target="tpu_custom_call" | custom-call | tf_op jit(solution)/shard_map/attention_backward/pallas_call | solution.py:279
  428.5 15.6 %convert_reduce_fusion.1 = (f32[3072]{0:T(1024)}, bf16[1024,3072]{1,0:T(8,128)(2,1)S(1)}) fusion(f32[1024,3072]{1,0:T(8,128)} %fusion.34, f32[3072]{0:T(1024)S(1)} %copy-done.163, bf16[1024,768]{1,0:T(8,128)(2,1)S(1)} %bitcast.449, bf16[3072,768]{1,0:T(8,128)(2,1)} %bitcast.406), kind=kOutput, calls=%fused_computation.21 | convolution fusion | flops 4904186880 | bytes 25190400 | tf_op jit(solution)/shard_map/dot_general | solution.py:55
  444.1 14.8 %convolution_convert_fusion = bf16[3072,768]{1,0:T(8,128)(2,1)} fusion(bf16[1024,768]{1,0:T(8,128)(2,1)S(1)} %bitcast.450, f32[1024,3072]{1,0:T(8,128)} %fusion.34, f32[3072]{0:T(1024)S(1)} %copy-done.163), kind=kOutput, calls=%fused_computation.25 | convolution fusion | flops 4865654784 | bytes 18886656 | tf_op jit(solution)/shard_map/dot_general | solution.py:49
  477.5 23.8 %attention_backward.3 = (bf16[1024,768]{1,0:T(8,128)(2,1)}, bf16[1024,768]{1,0:T(8,128)(2,1)}, bf16[1024,768]{1,0:T(8,128)(2,1)}) custom-call(bf16[1024,768]{1,0:T(8,128)(2,1)} %add_convert_fusion.9.queries_ref, bf16[1024,768]{1,0:T(8,128)(2,1)} %convolution_convert_fusion.7.keys_ref, bf16[1024,768]{1,0:T(8,128)(2,1)} %add_convert_fusion.8.values_ref, ...), custom_call_target="tpu_custom_call" | custom-call | tf_op jit(solution)/shard_map/attention_backward/pallas_call | solution.py:279
  582.4 14.2 %collective-permute-done.9 = bf16[4,4,10752]{2,0,1:T(4,128)(2,1)S(1)} collective-permute-done((bf16[4,4,10752]{2,0,1:T(4,128)(2,1)S(1)}, bf16[4,4,10752]{2,0,1:T(4,128)(2,1)S(1)}, u32[]{:S(2)}, u32[]{:S(2)}) %collective-permute-start.9) | collective-permute-done | bytes 344096 | tf_op jit(solution)/shard_map/ppermute | solution.py:120
  609.1 17.0 %collective-permute-done.10 = bf16[8,4,10752]{2,0,1:T(8,128)(2,1)} collective-permute-done((bf16[8,4,10752]{2,0,1:T(8,128)(2,1)}, bf16[8,4,10752]{2,0,1:T(8,128)(2,1)}, u32[]{:S(2)}, u32[]{:S(2)}) %collective-permute-start.10) | collective-permute-done | bytes 688160 | tf_op jit(solution)/shard_map/ppermute | solution.py:120
  626.1 8.3 concatenate.196
  661.6 9.3 %collective-permute-done.22 = f32[32,768]{1,0:T(8,128)S(1)} collective-permute-done((f32[32,768]{1,0:T(8,128)S(1)}, f32[32,768]{1,0:T(8,128)S(1)}, u32[]{:S(2)}, u32[]{:S(2)}) %collective-permute-start.22) | collective-permute-done | bytes 98336 | tf_op jit(solution)/shard_map/ppermute | solution.py:120
  671.7 14.9 %concatenate.197 = bf16[32,4,10752]{2,0,1:T(8,128)(2,1)S(1)} concatenate(bf16[1,4,10752]{2,0,1:T(2,128)(2,1)} %copy-done.43, bf16[1,4,10752]{2,0,1:T(2,128)(2,1)} %copy-done.45, bf16[1,4,10752]{2,0,1:T(2,128)(2,1)} %copy-done.47, bf16[1,4,10752]{2,0,1:T(2,128)(2,1)} %copy-done.48, bf16[4,4,10752]{2,0,1:T(4,128)(2,1)S(1)} %collective-permute-done.9, ...), dimensions={0} | concatenate | bytes 5505024 | tf_op jit(solution)/shard_map/concatenate | solution.py:129
  699.9 10.2 %add_convert_fusion = bf16[4,2,2,288,768]{4,3,0,2,1:T(8,128)(2,1)} fusion(bf16[4,2,2,288,768]{4,3,0,2,1:T(8,128)(2,1)} %collective-permute-done.23, bf16[4,2,2,288,768]{4,3,0,2,1:T(8,128)(2,1)} %bitcast_dynamic-update-slice_fusion.1), kind=kLoop, calls=%fused_computation.5 | loop fusion | flops 14155776 | bytes 21233664 | tf_op jit(solution)/shard_map/convert_element_type | solution.py:175
  730.4 25.9 %collective-permute-done.15 = bf16[4,24,128]{2,1,0:T(8,128)(2,1)S(1)} collective-permute-done((bf16[4,24,128]{2,1,0:T(8,128)(2,1)S(1)}, bf16[4,24,128]{2,1,0:T(8,128)(2,1)S(1)}, u32[]{:S(2)}, u32[]{:S(2)}) %collective-permute-start.15) | collective-permute-done | bytes 24608 | tf_op jit(solution)/shard_map/ppermute | solution.py:120
  806.1 13.9 %collective-permute-done.27 = bf16[144,768]{1,0:T(8,128)(2,1)S(1)} collective-permute-done((bf16[144,768]{1,0:T(8,128)(2,1)S(1)}, bf16[144,768]{1,0:T(8,128)(2,1)S(1)}, u32[]{:S(2)}, u32[]{:S(2)}) %collective-permute-start.27) | collective-permute-done | bytes 221216 | tf_op jit(solution)/shard_map/ppermute | solution.py:120
  824.0 8.7 collective-permute-done.32
  (806 shorter events, 505.1 us)
Async XLA Ops:
  7.2 125.5 %all-gather.3.cloned.1.call-start = ((), (), s32[]{:S(2)}) async-start(), calls=%async_computation.3 | async-start | bytes 14598144 | tf_op jit(solution)/shard_map/all_gather | solution.py:348
  12.5 225.7 %all-gather.5.cloned.1.call-start = ((), (), s32[]{:S(2)}) async-start(), calls=%async_computation.4 | async-start | bytes 14598144 | tf_op jit(solution)/shard_map/all_gather | solution.py:348
  47.2 27.5 %collective-permute-start.4 = (bf16[8,24,2096]{2,1,0:T(8,128)(2,1)}, bf16[8,24,2096]{2,1,0:T(8,128)(2,1)}, u32[]{:S(2)}, u32[]{:S(2)}) collective-permute-start(bf16[8,24,2096]{2,1,0:T(8,128)(2,1)} %get-tuple-element.200), channel_id=1, source_target_pairs={{0,4},{1,5},{2,6},{3,7},{4,0},{5,1},{6,2},{7,3},{8,12},{9,13},{10,... | collective-permute-start | bytes 2414600 | tf_op jit(solution)/shard_map/ppermute | solution.py:120
  55.7 43.8 %all-to-all-start = ((bf16[24,32,336]{2,0,1:T(8,128)(2,1)}), bf16[24,32,336]{2,0,1:T(8,128)(2,1)}, u32[]{:S(2)}, u32[]{:S(2)}) async-start(bf16[24,32,336]{2,0,1:T(8,128)(2,1)} %copy.308), calls=%async_computation | async-start | bytes 1179648 | tf_op jit(solution)/shard_map/all_to_all | solution.py:352
  101.6 16.6 %all-to-all-start.1 = ((f32[32,4,336]{2,1,0:T(4,128)}), f32[32,4,336]{2,1,0:T(4,128)S(1)}, u32[]{:S(2)}, u32[]{:S(2)}) async-start(f32[32,4,336]{2,1,0:T(4,128)} %copy.311), calls=%async_computation.1 | async-start | bytes 393216 | tf_op jit(solution)/shard_map/all_to_all | solution.py:399
  104.7 730.9 %reduce-scatter.2.cloned.1.call-start = ((), (), s32[]{:S(2)}) async-start(), calls=%async_computation.5 | async-start | bytes 14598144 | tf_op jit(solution)/shard_map/reduce_scatter | solution.py:545
  534.1 28.9 %collective-permute-start.6 = (bf16[1,4,10752]{2,0,1:T(2,128)(2,1)S(1)}, bf16[1,4,10752]{2,0,1:T(2,128)(2,1)S(1)}, u32[]{:S(2)}, u32[]{:S(2)}) collective-permute-start(bf16[1,4,10752]{2,0,1:T(2,128)(2,1)S(1)} %constant_dynamic-update-slice_fusion.45), channel_id=1, source_target_pairs={{0,8},{1,9},{2,10},{3,11},{4,12},{5,13},{6,14},{7,15},{8,16},{9,17... | collective-permute-start | bytes 258056 | tf_op jit(solution)/shard_map/ppermute | solution.py:120
  551.2 148.8 %collective-permute-start.23 = (bf16[4,2,2,288,768]{4,3,0,2,1:T(8,128)(2,1)}, bf16[4,2,2,288,768]{4,3,0,2,1:T(8,128)(2,1)}, u32[]{:S(2)}, u32[]{:S(2)}) collective-permute-start(bf16[4,2,2,288,768]{4,3,0,2,1:T(8,128)(2,1)} %bitcast_dynamic-update-slice_fusion), channel_id=1, source_target_pairs={{0,1},{1,0},{2,3},{3,2},{4,5},{5,4},{6,7},{7,6},{8,9},{9,8},{10,11... | collective-permute-start | bytes 21233672 | tf_op jit(solution)/shard_map/ppermute | solution.py:120
  561.6 75.4 %collective-permute-start.18 = (f32[32,768]{1,0:T(8,128)}, f32[32,768]{1,0:T(8,128)}, u32[]{:S(2)}, u32[]{:S(2)}) collective-permute-start(f32[32,768]{1,0:T(8,128)} %pad_maximum_fusion.12), channel_id=1, source_target_pairs={{0,1},{1,0},{2,3},{3,2},{4,5},{5,4},{6,7},{7,6},{8,9},{9,8},{10,11... | collective-permute-start | bytes 294920 | tf_op jit(solution)/shard_map/ppermute | solution.py:120
  579.1 17.5 %collective-permute-start.9 = (bf16[4,4,10752]{2,0,1:T(4,128)(2,1)S(1)}, bf16[4,4,10752]{2,0,1:T(4,128)(2,1)S(1)}, u32[]{:S(2)}, u32[]{:S(2)}) collective-permute-start(bf16[4,4,10752]{2,0,1:T(4,128)(2,1)S(1)} %pad_maximum_fusion.7), channel_id=1, source_target_pairs={{0,2},{1,3},{2,0},{3,1},{4,6},{5,7},{6,4},{7,5},{8,10},{9,11},{10,... | collective-permute-start | bytes 1032200 | tf_op jit(solution)/shard_map/ppermute | solution.py:120
  601.6 24.5 %collective-permute-start.10 = (bf16[8,4,10752]{2,0,1:T(8,128)(2,1)}, bf16[8,4,10752]{2,0,1:T(8,128)(2,1)}, u32[]{:S(2)}, u32[]{:S(2)}) collective-permute-start(bf16[8,4,10752]{2,0,1:T(8,128)(2,1)} %concatenate.195), channel_id=1, source_target_pairs={{0,4},{1,5},{2,6},{3,7},{4,0},{5,1},{6,2},{7,3},{8,12},{9,13},{10,... | collective-permute-start | bytes 2064392 | tf_op jit(solution)/shard_map/ppermute | solution.py:120
  634.5 37.2 %collective-permute-start.11 = (bf16[16,4,10752]{2,0,1:T(8,128)(2,1)}, bf16[16,4,10752]{2,0,1:T(8,128)(2,1)}, u32[]{:S(2)}, u32[]{:S(2)}) collective-permute-start(bf16[16,4,10752]{2,0,1:T(8,128)(2,1)} %concatenate.196), channel_id=1, source_target_pairs={{0,1},{1,0},{2,3},{3,2},{4,5},{5,4},{6,7},{7,6},{8,9},{9,8},{10,11... | collective-permute-start | bytes 4128776 | tf_op jit(solution)/shard_map/ppermute | solution.py:120
  660.6 10.2 %collective-permute-start.22 = (f32[32,768]{1,0:T(8,128)S(1)}, f32[32,768]{1,0:T(8,128)S(1)}, u32[]{:S(2)}, u32[]{:S(2)}) collective-permute-start(f32[32,768]{1,0:T(8,128)S(1)} %add.1086), channel_id=1, source_target_pairs={{0,16},{1,17},{2,18},{3,19},{4,20},{5,21},{6,22},{7,23},{8,24},{9,... | collective-permute-start | bytes 294920 | tf_op jit(solution)/shard_map/ppermute | solution.py:120
  697.6 21.1 %collective-permute-start.12 = (bf16[1,24,128]{2,1,0:T(8,128)(2,1)S(1)}, bf16[1,24,128]{2,1,0:T(8,128)(2,1)S(1)}, u32[]{:S(2)}, u32[]{:S(2)}) collective-permute-start(bf16[1,24,128]{2,1,0:T(8,128)(2,1)S(1)} %get-tuple-element.299), channel_id=1, source_target_pairs={{0,8},{1,9},{2,10},{3,11},{4,12},{5,13},{6,14},{7,15},{8,16},{9,17... | collective-permute-start | bytes 18440 | tf_op jit(solution)/shard_map/ppermute | solution.py:120
  715.3 48.2 %collective-permute-start.24 = (bf16[4,2,144,768]{3,2,0,1:T(8,128)(2,1)}, bf16[4,2,144,768]{3,2,0,1:T(8,128)(2,1)}, u32[]{:S(2)}, u32[]{:S(2)}) collective-permute-start(bf16[4,2,144,768]{3,2,0,1:T(8,128)(2,1)} %dynamic-slice_bitcast_fusion.1), channel_id=1, source_target_pairs={{0,2},{1,3},{2,0},{3,1},{4,6},{5,7},{6,4},{7,5},{8,10},{9,11},{10,... | collective-permute-start | bytes 5308424 | tf_op jit(solution)/shard_map/ppermute | solution.py:120
  717.3 50.0 %collective-permute-start.29 = (bf16[4,2,144,768]{3,2,0,1:T(8,128)(2,1)S(1)}, bf16[4,2,144,768]{3,2,0,1:T(8,128)(2,1)}, u32[]{:S(2)}, u32[]{:S(2)}) collective-permute-start(bf16[4,2,144,768]{3,2,0,1:T(8,128)(2,1)S(1)} %dynamic-slice_bitcast_fusion), channel_id=1, source_target_pairs={{0,4},{1,5},{2,6},{3,7},{4,0},{5,1},{6,2},{7,3},{8,12},{9,13},{10,... | collective-permute-start | bytes 5308424 | tf_op jit(solution)/shard_map/ppermute | solution.py:120
  729.6 26.7 %collective-permute-start.15 = (bf16[4,24,128]{2,1,0:T(8,128)(2,1)S(1)}, bf16[4,24,128]{2,1,0:T(8,128)(2,1)S(1)}, u32[]{:S(2)}, u32[]{:S(2)}) collective-permute-start(bf16[4,24,128]{2,1,0:T(8,128)(2,1)S(1)} %pad_maximum_fusion.17), channel_id=1, source_target_pairs={{0,2},{1,3},{2,0},{3,1},{4,6},{5,7},{6,4},{7,5},{8,10},{9,11},{10,... | collective-permute-start | bytes 73736 | tf_op jit(solution)/shard_map/ppermute | solution.py:120
  767.1 22.3 %collective-permute-start.25 = (bf16[4,144,768]{2,1,0:T(8,128)(2,1)}, bf16[4,144,768]{2,1,0:T(8,128)(2,1)}, u32[]{:S(2)}, u32[]{:S(2)}) collective-permute-start(bf16[4,144,768]{2,1,0:T(8,128)(2,1)} %dynamic-slice_bitcast_fusion.3), channel_id=1, source_target_pairs={{0,4},{1,5},{2,6},{3,7},{4,0},{5,1},{6,2},{7,3},{8,12},{9,13},{10,... | collective-permute-start | bytes 2654216 | tf_op jit(solution)/shard_map/ppermute | solution.py:120
  770.2 24.8 %collective-permute-start.30 = (bf16[4,144,768]{2,1,0:T(8,128)(2,1)}, bf16[4,144,768]{2,1,0:T(8,128)(2,1)}, u32[]{:S(2)}, u32[]{:S(2)}) collective-permute-start(bf16[4,144,768]{2,1,0:T(8,128)(2,1)} %dynamic-slice_bitcast_fusion.2), channel_id=1, source_target_pairs={{0,2},{1,3},{2,0},{3,1},{4,6},{5,7},{6,4},{7,5},{8,10},{9,11},{10,... | collective-permute-start | bytes 2654216 | tf_op jit(solution)/shard_map/ppermute | solution.py:120
  790.9 15.2 %collective-permute-start.28 = (bf16[144,768]{1,0:T(8,128)(2,1)S(1)}, bf16[144,768]{1,0:T(8,128)(2,1)S(1)}, u32[]{:S(2)}, u32[]{:S(2)}) collective-permute-start(bf16[144,768]{1,0:T(8,128)(2,1)S(1)} %get-tuple-element.172), channel_id=1, source_target_pairs={{0,24},{1,25},{2,26},{3,27},{4,28},{5,29},{6,30},{7,31},{8,0},{9,1... | collective-permute-start | bytes 663560 | tf_op jit(solution)/shard_map/ppermute | solution.py:120
  794.7 25.3 %collective-permute-start.27 = (bf16[144,768]{1,0:T(8,128)(2,1)S(1)}, bf16[144,768]{1,0:T(8,128)(2,1)S(1)}, u32[]{:S(2)}, u32[]{:S(2)}) collective-permute-start(bf16[144,768]{1,0:T(8,128)(2,1)S(1)} %get-tuple-element.173), channel_id=1, source_target_pairs={{0,16},{1,17},{2,18},{3,19},{4,20},{5,21},{6,22},{7,23},{8,24},{9,... | collective-permute-start | bytes 663560 | tf_op jit(solution)/shard_map/ppermute | solution.py:120
  796.4 27.6 %collective-permute-start.31 = (bf16[144,768]{1,0:T(8,128)(2,1)S(1)}, bf16[144,768]{1,0:T(8,128)(2,1)S(1)}, u32[]{:S(2)}, u32[]{:S(2)}) collective-permute-start(bf16[144,768]{1,0:T(8,128)(2,1)S(1)} %get-tuple-element.168), channel_id=1, source_target_pairs={{0,8},{1,9},{2,10},{3,11},{4,12},{5,13},{6,14},{7,15},{8,16},{9,17... | collective-permute-start | bytes 663560 | tf_op jit(solution)/shard_map/ppermute | solution.py:120
  798.5 25.5 %collective-permute-start.33 = (bf16[144,768]{1,0:T(8,128)(2,1)S(1)}, bf16[144,768]{1,0:T(8,128)(2,1)S(1)}, u32[]{:S(2)}, u32[]{:S(2)}) collective-permute-start(bf16[144,768]{1,0:T(8,128)(2,1)S(1)} %get-tuple-element.169), channel_id=1, source_target_pairs={{0,24},{1,25},{2,26},{3,27},{4,28},{5,29},{6,30},{7,31},{8,0},{9,1... | collective-permute-start | bytes 663560 | tf_op jit(solution)/shard_map/ppermute | solution.py:120
  801.0 31.8 %collective-permute-start.32 = (bf16[144,768]{1,0:T(8,128)(2,1)S(1)}, bf16[144,768]{1,0:T(8,128)(2,1)S(1)}, u32[]{:S(2)}, u32[]{:S(2)}) collective-permute-start(bf16[144,768]{1,0:T(8,128)(2,1)S(1)} %get-tuple-element.170), channel_id=1, source_target_pairs={{0,16},{1,17},{2,18},{3,19},{4,20},{5,21},{6,22},{7,23},{8,24},{9,... | collective-permute-start | bytes 663560 | tf_op jit(solution)/shard_map/ppermute | solution.py:120
  (220 other events, 1896.7 us)
Sparse Core Ops, SparseCore 0:
  12.6 120.0 all-gather.2
  136.2 101.9 all-gather.4
  521.2 171.3 reduce-scatter.1
